TPU v7x, 512 devices: a whole 4x8x8 slice. The times are simulated.
512 devices in a mesh: leaf: 64 (over x, y, core), grp: 8 (over z).
Axes of the slice: x: 4, y: 8, z: 8, core: 2. Of those that a mesh axis runs over, the one named last changes fastest.
Arguments:
- points: bfloat16 [256, 524288], P(None, ('leaf', 'grp')), may hold values from -6 to 6
- charges: bfloat16 [64, 524288], P(None, ('leaf', 'grp')), may hold values from -6 to 6
- order: int32 [524288], P(('leaf', 'grp')), may hold values from 0 to 1023, as said below
- near_mask: int32 [512, 5], P(('leaf', 'grp')), may hold values from 0 to 1, as said below
- skeletons: int32 [512, 7, 128], P(('leaf', 'grp')), may hold values from 0 to 1023, as said below
- leaf_interp: bfloat16 [128, 524288], P(None, ('leaf', 'grp')), may hold values from -0.5 to 0.5
- transfer: bfloat16 [512, 6, 128, 128], P(('leaf', 'grp')), as said below
Outputs:
- potentials: float32 [64, 524288], P(None, ('leaf', 'grp'))
Inputs may be any that keep to these rules, and one draw needn't show every extreme that they name: `order`: within each block of 1024 consecutive entries, a permutation of 0 to 1023. `near_mask`: entry 2 of every row is 1; an entry is 0 where it points outside the leaf coordinates; the pattern is symmetric: block b marks the block k leaf coordinates away exactly when that block marks b. Level 0 holds 128 different rows of the block; level j >= 1 holds 128 different positions of 0 to 255 in the two children's skeletons; the set of a node is the same on every block of that node. `transfer`: the matrix of a node is the same on every block of that node.
All inputs are finite; a program needn't handle non-finite values.
Results may differ from a plain program's by a relative error of at most 0.0019.
Values may be sent and summed in bfloat16 or wider, within the bound.
A program may use at most 64 MiB of HBM per device.

v0:
```python
import jax
import jax.numpy as jnp
from jax import lax
from jax.sharding import PartitionSpec as P

REACH = 2


HIGHEST_PRECISION = lax.Precision.HIGHEST


def passed_along(value, axis, steps):
    count = lax.axis_size(axis)
    initial, last = (max(0, -steps), min(count, count - steps))
    return lax.ppermute(value, axis, [(source, source + steps) for source in range(initial, last)])


def from_partner(block, axis, stride):
    count = lax.axis_size(axis)
    route = []
    for low in range(count):
        high = low | 1 << stride
        if high != low and high < count:
            route += [(low, high), (high, low)]
    return lax.ppermute(block, axis, route)


def pair_kernel(source, target):
    source_wide = source.astype(jnp.float32)
    target_wide = target.astype(jnp.float32)
    source_square = jnp.sum(source_wide * source_wide, axis=0)
    target_square = jnp.sum(target_wide * target_wide, axis=0)
    inner = lax.dot_general(
        source, target, (((0,), (0,)), ((), ())), preferred_element_type=jnp.float32
    )
    return jnp.exp(
        -2.0 * (source_square[:, None] + target_square[None, :] - 2.0 * inner) / source.shape[0]
    )


def apply_tile(source, source_charges, target):
    width = min(512, target.shape[1])
    outputs = []
    for column in range(0, target.shape[1], width):
        tile = pair_kernel(source, target[:, column : column + width]).astype(jnp.bfloat16)
        outputs.append(jnp.dot(source_charges, tile, preferred_element_type=jnp.float32))
    return jnp.concatenate(outputs, axis=1)


def local(points, charges, order, near_mask, skeletons, leaf_interp, transfer):
    dimension = points.shape[0]
    sides = charges.shape[0]
    leaf_rows = points.shape[1]
    ordered = jnp.take(charges, order, axis=1)
    packed = jnp.concatenate([points, ordered], axis=0)
    near_field = jnp.zeros((sides, leaf_rows), jnp.float32)
    for offset in range(-REACH, REACH + 1):
        if offset == 0:
            neighbour = packed
        else:
            neighbour = passed_along(packed, "leaf", -offset)

        def add_tile(carry, neighbour_data=neighbour):
            return carry + apply_tile(
                neighbour_data[:dimension], neighbour_data[dimension:], points
            )

        near_field = lax.cond(
            near_mask[0, offset + REACH] > 0, add_tile, lambda carry: carry, near_field
        )
    weights_now = lax.dot_general(
        ordered, leaf_interp, (((1,), (1,)), ((), ())), preferred_element_type=jnp.float32
    )
    coords = jnp.take(points, skeletons[0, 0], axis=1).astype(jnp.float32)
    levels = lax.axis_size("leaf").bit_length() - 1
    position = lax.axis_index("leaf")
    history = []
    for level in range(1, levels + 1):
        transfer_now = transfer[0, level - 1].astype(jnp.float32)
        contrib = jnp.dot(weights_now, transfer_now.T, precision=HIGHEST_PRECISION)
        bundle = jnp.concatenate([weights_now, contrib, coords], axis=0)
        partner = from_partner(bundle, "leaf", level - 1)
        partner_weights = partner[:sides]
        partner_contrib = partner[sides : 2 * sides]
        partner_coords = partner[2 * sides :]
        history.append((coords, partner_weights, partner_coords))
        upper_bit = position >> level - 1 & 1
        lower_first = jnp.concatenate([coords, partner_coords], axis=1)
        upper_first = jnp.concatenate([partner_coords, coords], axis=1)
        joined = jnp.where(upper_bit == 0, lower_first, upper_first)
        coords = jnp.take(joined, skeletons[0, level], axis=1)
        weights_now = contrib + partner_contrib
    top_bundle = jnp.concatenate([weights_now, coords], axis=0)[None]
    everyone = lax.all_gather(top_bundle.astype(jnp.bfloat16), "grp", axis=0, tiled=True).astype(
        top_bundle.dtype
    )
    other_weights = everyone[:, :sides]
    other_coords = everyone[:, sides:].astype(jnp.bfloat16)
    own_coords = coords.astype(jnp.bfloat16)
    kernels = jax.vmap(lambda source_coords: pair_kernel(source_coords, own_coords))(other_coords)
    keep = (jnp.arange(everyone.shape[0]) != lax.axis_index("grp")).astype(jnp.float32)
    potential = jnp.einsum(
        "hrk,hkm->rm", other_weights, kernels * keep[:, None, None], precision=HIGHEST_PRECISION
    )
    for level in range(levels, 0, -1):
        child_coords, sibling_weights, sibling_coords = history[level - 1]
        transfer_now = transfer[0, level - 1].astype(jnp.float32)
        sibling_kernel = pair_kernel(
            sibling_coords.astype(jnp.bfloat16), child_coords.astype(jnp.bfloat16)
        )
        potential = jnp.dot(potential, transfer_now, precision=HIGHEST_PRECISION) + jnp.dot(
            sibling_weights, sibling_kernel, precision=HIGHEST_PRECISION
        )
    far_field = jnp.dot(potential, leaf_interp.astype(jnp.float32), precision=HIGHEST_PRECISION)
    return near_field + far_field


def solution(mesh):
    in_specs = (
        P(None, ("leaf", "grp")),
        P(None, ("leaf", "grp")),
        P(("leaf", "grp")),
        P(("leaf", "grp"), None),
        P(("leaf", "grp"), None, None),
        P(None, ("leaf", "grp")),
        P(("leaf", "grp"), None, None, None),
    )
    out_specs = P(None, ("leaf", "grp"))
    return jax.shard_map(local, mesh=mesh, in_specs=in_specs, out_specs=out_specs, check_vma=False)
```

profile of v0, /device:TPU:16, one launch (start us, length us, event | category | flops | bytes accessed | tf_op | source)
XLA Modules:
  0.0 148.6 jit_solution(462891518636589742)
XLA Ops:
  1.4 1.1 copy.25
  2.5 3.2 %gather_fusion = bf16[1024,64]{1,0:T(8,128)(2,1)S(1)} fusion(bf16[64,1024]{0,1:T(8,128)(2,1)S(1)} %copy.25, s32[1024]{0:T(1024)S(1)} %fusion.207), kind=kCustom, calls=%fused_computation.6 | custom fusion | bytes 266240 | tf_op jit(solution)/shard_map/jit(_take)/gather | solution.py:54
  6.8 3.5 %collective-permute-start = (bf16[320,1024]{1,0:T(8,128)(2,1)S(1)}, bf16[320,1024]{1,0:T(8,128)(2,1)}, u32[]{:S(2)}, u32[]{:S(2)}) collective-permute-start(bf16[320,1024]{1,0:T(8,128)(2,1)S(1)} %pad_maximum_fusion.1), channel_id=1, source_target_pairs={{0,16},{8,24},{16,32},{24,40},{32,48},{40,56},{48,64},{56,72},{64,... | collective-permute-start | bytes 1966088 | tf_op jit(solution)/shard_map/ppermute | solution.py:15
  10.3 1.9 %collective-permute-start.1 = (bf16[320,1024]{1,0:T(8,128)(2,1)S(1)}, bf16[320,1024]{1,0:T(8,128)(2,1)}, u32[]{:S(2)}, u32[]{:S(2)}) collective-permute-start(bf16[320,1024]{1,0:T(8,128)(2,1)S(1)} %pad_maximum_fusion.1), channel_id=1, source_target_pairs={{0,8},{8,16},{16,24},{24,32},{32,40},{40,48},{48,56},{56,64},{64,7... | collective-permute-start | bytes 1966088 | tf_op jit(solution)/shard_map/ppermute | solution.py:15
  12.3 3.6 %collective-permute-start.2 = (bf16[320,1024]{1,0:T(8,128)(2,1)S(1)}, bf16[320,1024]{1,0:T(8,128)(2,1)}, u32[]{:S(2)}, u32[]{:S(2)}) collective-permute-start(bf16[320,1024]{1,0:T(8,128)(2,1)S(1)} %pad_maximum_fusion.1), channel_id=1, source_target_pairs={{8,0},{16,8},{24,16},{32,24},{40,32},{48,40},{56,48},{64,56},{72,6... | collective-permute-start | bytes 1966088 | tf_op jit(solution)/shard_map/ppermute | solution.py:15
  15.9 2.4 %collective-permute-start.3 = (bf16[320,1024]{1,0:T(8,128)(2,1)S(1)}, bf16[320,1024]{1,0:T(8,128)(2,1)}, u32[]{:S(2)}, u32[]{:S(2)}) collective-permute-start(bf16[320,1024]{1,0:T(8,128)(2,1)S(1)} %pad_maximum_fusion.1), channel_id=1, source_target_pairs={{16,0},{24,8},{32,16},{40,24},{48,32},{56,40},{64,48},{72,56},{80,... | collective-permute-start | bytes 1966088 | tf_op jit(solution)/shard_map/ppermute | solution.py:15
  20.8 2.6 %collective-permute-start.4 = (f32[384,128]{1,0:T(8,128)S(1)}, f32[384,128]{1,0:T(8,128)S(1)}, u32[]{:S(2)}, u32[]{:S(2)}) collective-permute-start(f32[384,128]{1,0:T(8,128)S(1)} %pad_maximum_fusion.2), channel_id=1, source_target_pairs={{0,8},{8,0},{16,24},{24,16},{32,40},{40,32},{48,56},{56,48},{64,72... | collective-permute-start | bytes 589832 | tf_op jit(solution)/shard_map/ppermute | solution.py:25
  29.5 3.7 %collective-permute-start.5 = (f32[384,128]{1,0:T(8,128)S(1)}, f32[384,128]{1,0:T(8,128)S(1)}, u32[]{:S(2)}, u32[]{:S(2)}) collective-permute-start(f32[384,128]{1,0:T(8,128)S(1)} %pad_maximum_fusion.3), channel_id=1, source_target_pairs={{0,16},{16,0},{8,24},{24,8},{32,48},{48,32},{40,56},{56,40},{64,80... | collective-permute-start | bytes 589832 | tf_op jit(solution)/shard_map/ppermute | solution.py:25
  33.4 12.1 %collective-permute-done.5 = f32[384,128]{1,0:T(8,128)S(1)} collective-permute-done((f32[384,128]{1,0:T(8,128)S(1)}, f32[384,128]{1,0:T(8,128)S(1)}, u32[]{:S(2)}, u32[]{:S(2)}) %collective-permute-start.5) | collective-permute-done | bytes 196640 | tf_op jit(solution)/shard_map/ppermute | solution.py:25
  47.4 1.9 %collective-permute-start.6 = (f32[384,128]{1,0:T(8,128)S(1)}, f32[384,128]{1,0:T(8,128)S(1)}, u32[]{:S(2)}, u32[]{:S(2)}) collective-permute-start(f32[384,128]{1,0:T(8,128)S(1)} %pad_maximum_fusion.4), channel_id=1, source_target_pairs={{0,32},{32,0},{8,40},{40,8},{16,48},{48,16},{24,56},{56,24},{64,96... | collective-permute-start | bytes 589832 | tf_op jit(solution)/shard_map/ppermute | solution.py:25
  49.6 6.4 %collective-permute-done.6 = f32[384,128]{1,0:T(8,128)S(1)} collective-permute-done((f32[384,128]{1,0:T(8,128)S(1)}, f32[384,128]{1,0:T(8,128)S(1)}, u32[]{:S(2)}, u32[]{:S(2)}) %collective-permute-start.6) | collective-permute-done | bytes 196640 | tf_op jit(solution)/shard_map/ppermute | solution.py:25
  59.1 3.5 %collective-permute-start.7 = (f32[384,128]{1,0:T(8,128)}, f32[384,128]{1,0:T(8,128)S(1)}, u32[]{:S(2)}, u32[]{:S(2)}) collective-permute-start(f32[384,128]{1,0:T(8,128)} %pad_maximum_fusion.5), channel_id=1, source_target_pairs={{0,64},{64,0},{8,72},{72,8},{16,80},{80,16},{24,88},{88,24},{32,96... | collective-permute-start | bytes 589832 | tf_op jit(solution)/shard_map/ppermute | solution.py:25
  62.8 6.8 %conditional.5 = (f32[64,1024]{1,0:T(8,128)S(1)}) conditional(s32[]{:T(128)} %bitcast.14, () %tuple.36, (bf16[320,1024]{1,0:T(8,128)(2,1)}, bf16[256,1024]{1,0:T(8,128)(2,1)S(1)}) %tuple.94), branch_computations={%region_0.1_spmd, %region_1.5_spmd} | conditional | flops 677967872 | bytes 3690504 | solution.py:68
  62.9 1.2 multiply_reduce_fusion
  64.1 2.0 %fusion.2 = f32[64,512]{1,0:T(8,128)S(1)} fusion(f32[512]{0:T(512)S(1)} %get-tuple-element.74, f32[1024]{0:T(1024)S(1)} %multiply_reduce_fusion, bf16[320,1024]{1,0:T(8,128)(2,1)} %get-tuple-element.52, bf16[256,1024]{1,0:T(8,128)(2,1)S(1)} %get-tuple-element.54), kind=kOutput, calls=%fused_computation.12 | convolution fusion | flops 338165760 | bytes 1054720 | tf_op jit(solution)/shard_map/cond/branch_1_fun/dot_general | solution.py:46
  66.1 2.6 %fusion.3 = f32[64,512]{1,0:T(8,128)} fusion(f32[512]{0:T(512)S(1)} %get-tuple-element.73, f32[1024]{0:T(1024)S(1)} %multiply_reduce_fusion, bf16[320,1024]{1,0:T(8,128)(2,1)} %get-tuple-element.52, bf16[256,1024]{1,0:T(8,128)(2,1)S(1)} %get-tuple-element.54), kind=kOutput, calls=%fused_computation.13 | convolution fusion | flops 338165760 | bytes 1054720 | tf_op jit(solution)/shard_map/cond/branch_1_fun/dot_general | solution.py:46
  69.6 6.9 %conditional.6 = (f32[64,1024]{1,0:T(8,128)S(1)}) conditional(s32[]{:T(128)} %bitcast.13, f32[64,1024]{1,0:T(8,128)S(1)} %get-tuple-element.139, (bf16[320,1024]{1,0:T(8,128)(2,1)}, bf16[256,1024]{1,0:T(8,128)(2,1)S(1)}, f32[64,1024]{1,0:T(8,128)S(1)}) %tuple.95), branch_computations={%region_5.6_spmd, %region_6.10_spmd} | conditional | flops 678033408 | bytes 3952648 | solution.py:68
  69.8 1.2 multiply_reduce_fusion.3
  71.0 2.0 %fusion.28 = f32[64,512]{1,0:T(8,128)S(1)} fusion(f32[512]{0:T(512)S(1)} %get-tuple-element.76, f32[1024]{0:T(1024)S(1)} %multiply_reduce_fusion.3, bf16[320,1024]{1,0:T(8,128)(2,1)} %get-tuple-element.56, bf16[256,1024]{1,0:T(8,128)(2,1)S(1)} %get-tuple-element.57), kind=kOutput, calls=%fused_computation.40 | convolution fusion | flops 338165760 | bytes 1054720 | tf_op jit(solution)/shard_map/cond/branch_1_fun/dot_general | solution.py:46
  72.9 2.6 %fusion.29 = f32[64,512]{1,0:T(8,128)} fusion(f32[512]{0:T(512)S(1)} %get-tuple-element.75, f32[1024]{0:T(1024)S(1)} %multiply_reduce_fusion.3, bf16[320,1024]{1,0:T(8,128)(2,1)} %get-tuple-element.56, bf16[256,1024]{1,0:T(8,128)(2,1)S(1)} %get-tuple-element.57), kind=kOutput, calls=%fused_computation.41 | convolution fusion | flops 338165760 | bytes 1054720 | tf_op jit(solution)/shard_map/cond/branch_1_fun/dot_general | solution.py:46
  75.6 1.0 maximum_add_fusion
  76.5 3.6 %conditional.7 = (f32[64,1024]{1,0:T(8,128)S(1)}) conditional(s32[]{:T(128)} %bitcast.12, f32[64,1024]{1,0:T(8,128)S(1)} %get-tuple-element.140, (bf16[256,1024]{1,0:T(8,128)(2,1)S(1)}, bf16[64,1024]{0,1:T(8,128)(2,1)S(1)}, f32[64,1024]{1,0:T(8,128)S(1)}) %tuple.96), branch_computations={%region_10.11_spmd, %region_11.15_spmd} | conditional | flops 678033408 | bytes 4214792 | solution.py:68
  77.7 1.5 %fusion.55 = f32[64,512]{1,0:T(8,128)} fusion(bf16[64,1024]{0,1:T(8,128)(2,1)S(1)} %get-tuple-element.71, bf16[256,1024]{1,0:T(8,128)(2,1)S(1)} %get-tuple-element.59, f32[512]{0:T(512)S(1)} %get-tuple-element.77, f32[1024]{0:T(1024)S(1)} %multiply_reduce_fusion.6), kind=kOutput, calls=%fused_computation.69 | convolution fusion | flops 338165760 | bytes 1185792 | tf_op jit(solution)/shard_map/cond/branch_1_fun/dot_general | solution.py:46
  80.2 5.3 %conditional.8 = (f32[64,1024]{1,0:T(8,128)S(1)}) conditional(s32[]{:T(128)} %bitcast.11, f32[64,1024]{1,0:T(8,128)S(1)} %get-tuple-element.141, (bf16[320,1024]{1,0:T(8,128)(2,1)}, bf16[256,1024]{1,0:T(8,128)(2,1)S(1)}, f32[64,1024]{1,0:T(8,128)S(1)}) %tuple.97), branch_computations={%region_15.16_spmd, %region_16.20_spmd} | conditional | flops 678033408 | bytes 3952648 | solution.py:68
  80.3 1.2 multiply_reduce_fusion.9
  81.5 2.0 %fusion.74 = f32[64,512]{1,0:T(8,128)S(1)} fusion(f32[512]{0:T(512)S(1)} %get-tuple-element.80, f32[1024]{0:T(1024)S(1)} %multiply_reduce_fusion.9, bf16[320,1024]{1,0:T(8,128)(2,1)} %get-tuple-element.62, bf16[256,1024]{1,0:T(8,128)(2,1)S(1)} %get-tuple-element.63), kind=kOutput, calls=%fused_computation.92 | convolution fusion | flops 338165760 | bytes 1054720 | tf_op jit(solution)/shard_map/cond/branch_1_fun/dot_general | solution.py:46
  83.5 2.0 %fusion.75 = f32[64,512]{1,0:T(8,128)S(1)} fusion(f32[512]{0:T(512)S(1)} %get-tuple-element.79, f32[1024]{0:T(1024)S(1)} %multiply_reduce_fusion.9, bf16[320,1024]{1,0:T(8,128)(2,1)} %get-tuple-element.62, bf16[256,1024]{1,0:T(8,128)(2,1)S(1)} %get-tuple-element.63), kind=kOutput, calls=%fused_computation.93 | convolution fusion | flops 338165760 | bytes 1054720 | tf_op jit(solution)/shard_map/cond/branch_1_fun/dot_general | solution.py:46
  87.1 1.9 %collective-permute-start.8 = (f32[384,128]{1,0:T(8,128)S(1)}, f32[384,128]{1,0:T(8,128)S(1)}, u32[]{:S(2)}, u32[]{:S(2)}) collective-permute-start(f32[384,128]{1,0:T(8,128)S(1)} %pad_maximum_fusion.6), channel_id=1, source_target_pairs={{0,128},{128,0},{8,136},{136,8},{16,144},{144,16},{24,152},{152,24... | collective-permute-start | bytes 589832 | tf_op jit(solution)/shard_map/ppermute | solution.py:25
  89.3 5.4 %collective-permute-done.8 = f32[384,128]{1,0:T(8,128)S(1)} collective-permute-done((f32[384,128]{1,0:T(8,128)S(1)}, f32[384,128]{1,0:T(8,128)S(1)}, u32[]{:S(2)}, u32[]{:S(2)}) %collective-permute-start.8) | collective-permute-done | bytes 196640 | tf_op jit(solution)/shard_map/ppermute | solution.py:25
  96.1 1.9 %collective-permute-start.9 = (f32[384,128]{1,0:T(8,128)S(1)}, f32[384,128]{1,0:T(8,128)S(1)}, u32[]{:S(2)}, u32[]{:S(2)}) collective-permute-start(f32[384,128]{1,0:T(8,128)S(1)} %pad_maximum_fusion.7), channel_id=1, source_target_pairs={{0,256},{256,0},{8,264},{264,8},{16,272},{272,16},{24,280},{280,24... | collective-permute-start | bytes 589832 | tf_op jit(solution)/shard_map/ppermute | solution.py:25
  98.2 6.9 %collective-permute-done.9 = f32[384,128]{1,0:T(8,128)S(1)} collective-permute-done((f32[384,128]{1,0:T(8,128)S(1)}, f32[384,128]{1,0:T(8,128)S(1)}, u32[]{:S(2)}, u32[]{:S(2)}) %collective-permute-start.9) | collective-permute-done | bytes 196640 | tf_op jit(solution)/shard_map/ppermute | solution.py:25
  106.7 37.6 %all_gather.3 = bf16[8,320,128]{2,1,0:T(8,128)(2,1)S(1)} all-gather(bf16[1,320,128]{2,1,0:T(8,128)(2,1)S(1)} %copy.42), channel_id=1, replica_groups=mesh['leaf'=64,'grp'=8] {'grp'}, dimensions={0}, use_global_device_ids=true | all-gather | bytes 737280 | tf_op jit(solution)/shard_map/all_gather | solution.py:94
  (145 shorter events, 25.8 us)
Async XLA Ops:
  0.0 20.1 %copy-start = (bf16[128,1024]{1,0:T(8,128)(2,1)S(1)}, bf16[128,1024]{1,0:T(8,128)(2,1)}, u32[]{:S(2)}) copy-start(bf16[128,1024]{1,0:T(8,128)(2,1)} %param.24) | copy-start | bytes 786436
  5.7 1.0 copy-start.1
  6.8 11.7 %copy-start.4 = (s32[1,7,128]{2,0,1:T(1,128)S(1)}, s32[1,7,128]{2,0,1:T(1,128)}, u32[]{:S(2)}) copy-start(s32[1,7,128]{2,0,1:T(1,128)} %param.23) | copy-start | bytes 10756
  6.8 56.0 %collective-permute-start = (bf16[320,1024]{1,0:T(8,128)(2,1)S(1)}, bf16[320,1024]{1,0:T(8,128)(2,1)}, u32[]{:S(2)}, u32[]{:S(2)}) collective-permute-start(bf16[320,1024]{1,0:T(8,128)(2,1)S(1)} %pad_maximum_fusion.1), channel_id=1, source_target_pairs={{0,16},{8,24},{16,32},{24,40},{32,48},{40,56},{48,64},{56,72},{64,... | collective-permute-start | bytes 1966088 | tf_op jit(solution)/shard_map/ppermute | solution.py:15
  10.3 59.3 %collective-permute-start.1 = (bf16[320,1024]{1,0:T(8,128)(2,1)S(1)}, bf16[320,1024]{1,0:T(8,128)(2,1)}, u32[]{:S(2)}, u32[]{:S(2)}) collective-permute-start(bf16[320,1024]{1,0:T(8,128)(2,1)S(1)} %pad_maximum_fusion.1), channel_id=1, source_target_pairs={{0,8},{8,16},{16,24},{24,32},{32,40},{40,48},{48,56},{56,64},{64,7... | collective-permute-start | bytes 1966088 | tf_op jit(solution)/shard_map/ppermute | solution.py:15
  12.3 67.9 %collective-permute-start.2 = (bf16[320,1024]{1,0:T(8,128)(2,1)S(1)}, bf16[320,1024]{1,0:T(8,128)(2,1)}, u32[]{:S(2)}, u32[]{:S(2)}) collective-permute-start(bf16[320,1024]{1,0:T(8,128)(2,1)S(1)} %pad_maximum_fusion.1), channel_id=1, source_target_pairs={{8,0},{16,8},{24,16},{32,24},{40,32},{48,40},{56,48},{64,56},{72,6... | collective-permute-start | bytes 1966088 | tf_op jit(solution)/shard_map/ppermute | solution.py:15
  15.9 69.6 %collective-permute-start.3 = (bf16[320,1024]{1,0:T(8,128)(2,1)S(1)}, bf16[320,1024]{1,0:T(8,128)(2,1)}, u32[]{:S(2)}, u32[]{:S(2)}) collective-permute-start(bf16[320,1024]{1,0:T(8,128)(2,1)S(1)} %pad_maximum_fusion.1), channel_id=1, source_target_pairs={{16,0},{24,8},{32,16},{40,24},{48,32},{56,40},{64,48},{72,56},{80,... | collective-permute-start | bytes 1966088 | tf_op jit(solution)/shard_map/ppermute | solution.py:15
  19.1 1.4 copy-start.2
  20.1 3.3 %copy-start.3 = (s32[1,5]{1,0:T(1,128)S(1)}, s32[1,5]{1,0:T(1,128)}, u32[]{:S(2)}) copy-start(s32[1,5]{1,0:T(1,128)} %param.22) | copy-start | bytes 64
  20.8 6.9 %collective-permute-start.4 = (f32[384,128]{1,0:T(8,128)S(1)}, f32[384,128]{1,0:T(8,128)S(1)}, u32[]{:S(2)}, u32[]{:S(2)}) collective-permute-start(f32[384,128]{1,0:T(8,128)S(1)} %pad_maximum_fusion.2), channel_id=1, source_target_pairs={{0,8},{8,0},{16,24},{24,16},{32,40},{40,32},{48,56},{56,48},{64,72... | collective-permute-start | bytes 589832 | tf_op jit(solution)/shard_map/ppermute | solution.py:25
  29.5 16.0 %collective-permute-start.5 = (f32[384,128]{1,0:T(8,128)S(1)}, f32[384,128]{1,0:T(8,128)S(1)}, u32[]{:S(2)}, u32[]{:S(2)}) collective-permute-start(f32[384,128]{1,0:T(8,128)S(1)} %pad_maximum_fusion.3), channel_id=1, source_target_pairs={{0,16},{16,0},{8,24},{24,8},{32,48},{48,32},{40,56},{56,40},{64,80... | collective-permute-start | bytes 589832 | tf_op jit(solution)/shard_map/ppermute | solution.py:25
  45.7 1.1 copy-start.13
  46.5 2.9 %copy-start.6 = (f32[128]{0:T(128)S(1)}, f32[128]{0:T(128)}, u32[]{:S(2)}) copy-start(f32[128]{0:T(128)} %get-tuple-element.83) | copy-start | bytes 1540
  47.4 8.6 %collective-permute-start.6 = (f32[384,128]{1,0:T(8,128)S(1)}, f32[384,128]{1,0:T(8,128)S(1)}, u32[]{:S(2)}, u32[]{:S(2)}) collective-permute-start(f32[384,128]{1,0:T(8,128)S(1)} %pad_maximum_fusion.4), channel_id=1, source_target_pairs={{0,32},{32,0},{8,40},{40,8},{16,48},{48,16},{24,56},{56,24},{64,96... | collective-permute-start | bytes 589832 | tf_op jit(solution)/shard_map/ppermute | solution.py:25
  56.9 0.9 copy-start.12
  57.7 4.9 %copy-start.7 = (f32[128]{0:T(128)S(1)}, f32[128]{0:T(128)}, u32[]{:S(2)}) copy-start(f32[128]{0:T(128)} %get-tuple-element.85) | copy-start | bytes 1540
  57.7 4.9 %copy-start.8 = (f32[128]{0:T(128)S(1)}, f32[128]{0:T(128)}, u32[]{:S(2)}) copy-start(f32[128]{0:T(128)} %get-tuple-element.111) | copy-start | bytes 1540
  59.1 26.7 %collective-permute-start.7 = (f32[384,128]{1,0:T(8,128)}, f32[384,128]{1,0:T(8,128)S(1)}, u32[]{:S(2)}, u32[]{:S(2)}) collective-permute-start(f32[384,128]{1,0:T(8,128)} %pad_maximum_fusion.5), channel_id=1, source_target_pairs={{0,64},{64,0},{8,72},{72,8},{16,80},{80,16},{24,88},{88,24},{32,96... | collective-permute-start | bytes 589832 | tf_op jit(solution)/shard_map/ppermute | solution.py:25
  86.2 0.9 copy-start.11
  86.9 2.1 %copy-start.5 = (f32[128]{0:T(128)S(1)}, f32[128]{0:T(128)}, u32[]{:S(2)}) copy-start(f32[128]{0:T(128)} %get-tuple-element.87) | copy-start | bytes 1540
  87.1 7.6 %collective-permute-start.8 = (f32[384,128]{1,0:T(8,128)S(1)}, f32[384,128]{1,0:T(8,128)S(1)}, u32[]{:S(2)}, u32[]{:S(2)}) collective-permute-start(f32[384,128]{1,0:T(8,128)S(1)} %pad_maximum_fusion.6), channel_id=1, source_target_pairs={{0,128},{128,0},{8,136},{136,8},{16,144},{144,16},{24,152},{152,24... | collective-permute-start | bytes 589832 | tf_op jit(solution)/shard_map/ppermute | solution.py:25
  95.1 0.9 copy-start.10
  96.1 9.1 %collective-permute-start.9 = (f32[384,128]{1,0:T(8,128)S(1)}, f32[384,128]{1,0:T(8,128)S(1)}, u32[]{:S(2)}, u32[]{:S(2)}) collective-permute-start(f32[384,128]{1,0:T(8,128)S(1)} %pad_maximum_fusion.7), channel_id=1, source_target_pairs={{0,256},{256,0},{8,264},{264,8},{16,272},{272,16},{24,280},{280,24... | collective-permute-start | bytes 589832 | tf_op jit(solution)/shard_map/ppermute | solution.py:25
  105.3 1.0 copy-start.9
  106.7 37.7 %copy-start.14 = (f32[8]{0:T(128)S(1)}, f32[8]{0:T(128)}, u32[]{:S(2)}) copy-start(f32[8]{0:T(128)} %compare_convert_fusion) | copy-start | bytes 100
where the time goes:
time: 150 us; the launch traced here: 149 us
  blocking collectives  37.6 us (25%)
  waiting for transfers between devices  30.8 us (21%)
  starting transfers between devices  27 us (18%)
  matrix products  21.3 us (14%)
  other arithmetic  14.6 us (10%)
  local copies, waits for them, and re-layouts  13 us (9%)
  between operations  3.87 us (3%)
    all_gather x1, blocking collectives, local(): lax.all_gather(top_bundle.astype(jnp.bfloat16), 'grp', axis=0, tiled=True)  37.6 us
    ppermute x6, waiting for transfers between devices, from_partner(): return lax.ppermute(block, axis, route)  30.8 us
    ppermute x6, starting transfers between devices, from_partner(): return lax.ppermute(block, axis, route)  15.5 us
    dot_general x8, matrix products, apply_tile(): jnp.dot(source_charges, tile, preferred_element_type=jnp.float32)  15.5 us
    ppermute x4, starting transfers between devices, passed_along(): lax.ppermute(value, axis, [(source, source + steps) for source in range(i...  11.4 us
    gather x11, local copies, waits for them, and re-layouts, local(): coords = jnp.take(joined, skeletons[0, level], axis=1)  5.06 us
    reduce_sum x11, other arithmetic, pair_kernel(): source_square = jnp.sum(source_wide * source_wide, axis=0)  4.54 us
    gather x1, local copies, waits for them, and re-layouts, local(): ordered = jnp.take(charges, order, axis=1)  3.21 us
  transfers between devices with their start and end apart: 10, of which 4 were waited for; matrix products, arithmetic and copies ran while one was open for 23% of the time, Pallas kernels for 0%

commit v1 on v0

v1 whole, which is shorter than its diff:
```python
import functools
import math

import jax
import jax.numpy as jnp
from jax import lax
from jax.experimental import pallas as pl
from jax.experimental.pallas import tpu as pltpu
from jax.sharding import PartitionSpec as P

MESH = pl.DeviceIdType.MESH
F32 = jnp.float32
BF16 = jnp.bfloat16
DIM, RHS, SK, LEAF, LEVELS = 256, 64, 128, 1024, 6
HALF_DIM, HALF_RHS = DIM // 2, RHS // 2
CONTRIB, COORD, WEIGHT, BUNDLE = 0, 2 * HALF_RHS, 2 * HALF_RHS + HALF_DIM, 4 * HALF_RHS + HALF_DIM
TOP = HALF_DIM + HALF_RHS
SCALE = 2.0 / DIM / math.log(2.0)
CHUNK = 256


def dot(a, b):
    return jnp.dot(a, b, preferred_element_type=F32)


def dot_nt(a, b):
    return lax.dot_general(a, b, (((1,), (1,)), ((), ())), preferred_element_type=F32)


def split(value):
    high = value.astype(BF16)
    low = (value - high.astype(F32)).astype(BF16)
    return high, low


def pair_kernel(source_t, target):
    wide_s = source_t.astype(F32)
    wide_t = target.astype(F32)
    square_s = jnp.sum(wide_s * wide_s, axis=1, keepdims=True) * SCALE
    square_t = jnp.sum(wide_t * wide_t, axis=0, keepdims=True) * SCALE
    return jnp.exp2(dot(source_t, target) * (2.0 * SCALE) - (square_s + square_t))


def kernel(
    n_y, n_x, n_grp,
    points_hbm, charges_hbm, order_hbm, mask_ref, skel_hbm, interp_hbm, transfer_hbm,
    out_ref,
    pts, chg, order, skel, interp, transfer,
    pts_t, ordered, norm_t, near_pts, near_chg, near,
    own, sib, top, far,
    load_sem, send_sem, recv_sem,
):
    leaf = lax.axis_index("leaf")
    grp = lax.axis_index("grp")
    core = leaf % 2
    other = 1 - core
    chip = leaf // 2
    y = chip % n_y
    x = chip // n_y
    n_chip = n_x * n_y
    has_a = chip > 0
    has_b = chip < n_chip - 1
    quad = y % 4

    def at_yx(yy, xx):
        return ((xx * n_y + (yy + n_y) % n_y) * 2 + core, grp)

    partner = (chip * 2 + other, grp)

    loads = [
        pltpu.make_async_copy(src, dst, load_sem.at[i])
        for i, (src, dst) in enumerate(
            [
                (order_hbm, order),
                (charges_hbm, chg),
                (interp_hbm, interp),
                (skel_hbm, skel),
                (points_hbm, pts),
                (transfer_hbm, transfer),
            ]
        )
    ]
    for load in loads:
        load.start()

    barrier = pltpu.get_barrier_semaphore()
    peers = [
        partner,
        at_yx(y + 1, x),
        at_yx(y - 1, x),
        at_yx(y + 2, x),
        at_yx(y - 2, x),
        at_yx(y, x ^ 1),
        at_yx(y, n_x - 1 - x),
    ]
    for step in range(1, n_grp):
        peers.append((leaf, (grp + step) % n_grp))
    for peer in peers:
        pl.semaphore_signal(barrier, inc=1, device_id=peer, device_id_type=MESH)

    @pl.when(has_a)
    def _():
        pl.semaphore_signal(barrier, inc=1, device_id=(leaf - 2, grp), device_id_type=MESH)

    @pl.when(has_b)
    def _():
        pl.semaphore_signal(barrier, inc=1, device_id=(leaf + 2, grp), device_id_type=MESH)

    def remote(src, dst, send, recv, device):
        return pltpu.make_async_remote_copy(
            src_ref=src,
            dst_ref=dst,
            send_sem=send_sem.at[send],
            recv_sem=recv_sem.at[recv],
            device_id=device,
            device_id_type=MESH,
        )

    loads[0].wait()
    loads[1].wait()
    for column in range(0, LEAF, CHUNK):
        wanted = order[:, column : column + CHUNK]
        rows = lax.broadcasted_iota(jnp.int32, (LEAF, CHUNK), 0)
        pick = jnp.where(rows == wanted, 1.0, 0.0).astype(BF16)
        ordered[:, column : column + CHUNK] = dot(chg[...], pick).astype(BF16)
    loads[2].wait()
    weights = dot_nt(ordered[...], interp[...])
    loads[3].wait()
    loads[4].wait()
    rows = lax.broadcasted_iota(jnp.int32, (LEAF, SK), 0)
    pick = jnp.where(rows == skel[0:1, :], 1.0, 0.0).astype(BF16)
    coords = dot(pts[...], pick).astype(BF16)
    loads[5].wait()

    def contribution(weights, level):
        high, low = split(weights)
        both = dot_nt(jnp.concatenate([high, low], axis=0), transfer[level])
        count = weights.shape[0]
        return high, low, both[:count] + both[count:]

    high, low, contrib = contribution(weights, 0)
    contrib_high, contrib_low = split(contrib)
    for half in range(2):
        part = slice(half * HALF_RHS, (half + 1) * HALF_RHS)
        own[0, half, 0:HALF_RHS] = contrib_high[part]
        own[0, half, HALF_RHS:COORD] = contrib_low[part]
        own[0, half, COORD:WEIGHT] = coords[half * HALF_DIM : (half + 1) * HALF_DIM]
        own[0, half, WEIGHT : WEIGHT + HALF_RHS] = high[part]
        own[0, half, WEIGHT + HALF_RHS : BUNDLE] = low[part]

    expected = len(peers) + has_a.astype(jnp.int32) + has_b.astype(jnp.int32)
    pl.semaphore_wait(barrier, expected)

    first = remote(own.at[0], sib.at[0], 0, 0, partner)
    first.start()
    for row in range(0, LEAF, CHUNK):
        pts_t[row : row + CHUNK, :] = jnp.transpose(pts[:, row : row + CHUNK])
    near_p = [
        remote(pts_t, near_pts.at[0], 1, 1, partner),
        remote(ordered, near_chg.at[0], 2, 2, partner),
    ]
    for copy in near_p:
        copy.start()
    wide = pts[...].astype(F32)
    norm_t[...] = jnp.sum(wide * wide, axis=0, keepdims=True) * SCALE
    near[...] = jnp.zeros_like(near)

    def near_tile(source_t, source_chg, keep):
        def body(step, carry):
            rows = pl.ds(pl.multiple_of(step * CHUNK, CHUNK), CHUNK)
            lhs = source_t[rows, :]
            wide = lhs.astype(F32)
            norm_s = jnp.sum(wide * wide, axis=1, keepdims=True) * SCALE
            charge = source_chg[:, rows]
            if keep is not None:
                charge = jnp.where(keep > 0, charge, jnp.zeros_like(charge))
            inner = dot(lhs, pts[...])
            tile = jnp.exp2(inner * (2.0 * SCALE) - (norm_s + norm_t[...])).astype(BF16)
            near[...] += dot(charge, tile)
            return carry

        lax.fori_loop(0, LEAF // CHUNK, body, 0)

    bits = [core, y % 2, (y // 2) % 2, (y // 4) % 2, x % 2, (x // 2) % 2]

    def selection(level):
        wanted = skel[level + 1 : level + 2, :]
        rows = lax.broadcasted_iota(jnp.int32, (SK, SK), 0)
        upper = bits[level] * SK
        mine = jnp.where(rows + upper == wanted, 1.0, 0.0).astype(BF16)
        theirs = jnp.where(rows + (SK - upper) == wanted, 1.0, 0.0).astype(BF16)
        return mine, theirs

    def joined_coords(level, half, picks):
        mine, theirs = picks
        picked = dot(own[level, half, COORD:WEIGHT, :], mine) + dot(
            sib[level, half, COORD:WEIGHT, :], theirs
        )
        return picked.astype(BF16)

    def summed_weights(level, half):
        total = own[level, half, 0:HALF_RHS].astype(F32) + own[
            level, half, HALF_RHS:COORD
        ].astype(F32)
        return (
            total
            + sib[level, half, 0:HALF_RHS].astype(F32)
            + sib[level, half, HALF_RHS:COORD].astype(F32)
        )

    def raise_level(level):
        own[level + 1, core, COORD:WEIGHT] = joined_coords(level, core, selection(level))
        weights = summed_weights(level, core)
        if level + 1 < LEVELS:
            high, low, contrib = contribution(weights, level + 1)
            contrib_high, contrib_low = split(contrib)
            own[level + 1, core, 0:HALF_RHS] = contrib_high
            own[level + 1, core, HALF_RHS:COORD] = contrib_low
            own[level + 1, core, WEIGHT : WEIGHT + HALF_RHS] = high
            own[level + 1, core, WEIGHT + HALF_RHS : BUNDLE] = low
        else:
            own[level + 1, core, WEIGHT : WEIGHT + HALF_RHS] = weights.astype(BF16)

    def raise_rest(level):
        own[level + 1, other, COORD:WEIGHT] = joined_coords(level, other, selection(level))

    def sibling_field(level):
        source = jnp.concatenate(
            [sib[level, 0, COORD:WEIGHT, :], sib[level, 1, COORD:WEIGHT, :]], axis=0
        )
        target = jnp.concatenate(
            [own[level, 0, COORD:WEIGHT, :], own[level, 1, COORD:WEIGHT, :]], axis=0
        )
        kern_high, kern_low = split(pair_kernel(jnp.transpose(source), target))
        high = jnp.concatenate(
            [sib[level, half, WEIGHT : WEIGHT + HALF_RHS, :] for half in range(2)], axis=0
        )
        low = jnp.concatenate(
            [sib[level, half, WEIGHT + HALF_RHS : BUNDLE, :] for half in range(2)], axis=0
        )
        both = dot(jnp.concatenate([high, low], axis=0), kern_high)
        far[level] = both[:RHS] + both[RHS:] + dot(high, kern_low)

    routes = {
        1: [(None, at_yx(y ^ 1, x))],
        2: [
            (quad == 1, at_yx(y + 2, x)),
            (quad == 1, at_yx(y + 1, x)),
            (quad == 2, at_yx(y - 2, x)),
            (quad == 2, at_yx(y - 1, x)),
        ],
        3: [
            (quad == 3, at_yx(y + 2, x)),
            (quad == 3, at_yx(y + 1, x)),
            (quad == 0, at_yx(y - 2, x)),
            (quad == 0, at_yx(y - 1, x)),
        ],
        4: [(None, at_yx(y, x ^ 1))],
        5: [(None, at_yx(y, n_x - 1 - x))],
    }

    def when(condition, action):
        if condition is None:
            action()
        else:
            pl.when(condition)(action)

    def bundle_copies(level):
        main, rest = [], []
        for index, (condition, device) in enumerate(routes[level]):
            base = 3 + (level - 1) * 8 + (index % 2) * 2
            recv = 3 + (level - 1) * 2
            source, target = own.at[level, core], sib.at[level, core]
            main.append(
                (
                    condition,
                    remote(
                        source.at[pl.ds(0, WEIGHT), :],
                        target.at[pl.ds(0, WEIGHT), :],
                        base,
                        recv,
                        device,
                    ),
                )
            )
            rest.append(
                (
                    condition,
                    remote(
                        source.at[pl.ds(WEIGHT, 2 * HALF_RHS), :],
                        target.at[pl.ds(WEIGHT, 2 * HALF_RHS), :],
                        base + 1,
                        recv + 1,
                        device,
                    ),
                )
            )
        return main, rest

    copies = {level: bundle_copies(level) for level in routes}

    def forward(level):
        part = pl.ds(COORD, BUNDLE - COORD)
        return remote(
            sib.at[level, core].at[part, :],
            sib.at[level, core].at[part, :],
            43 + level,
            13 + level,
            partner,
        )

    def forwarded(level):
        part = pl.ds(COORD, BUNDLE - COORD)
        return remote(
            sib.at[level, other].at[part, :],
            sib.at[level, other].at[part, :],
            43 + level,
            13 + level,
            partner,
        )

    def send_level(level):
        for condition, copy in copies[level][0] + copies[level][1]:
            when(condition, copy.start)

    def finish_sends(level):
        for condition, copy in copies[level][0] + copies[level][1]:
            when(condition, copy.wait_send)

    first.wait_recv()
    raise_level(0)
    send_level(1)
    raise_rest(0)
    sibling_field(0)

    near_tile(pts_t, ordered, None)

    def receive_main(level):
        copies[level][0][0][1].wait_recv()

    def receive_rest(level):
        copies[level][1][0][1].wait_recv()
        forward(level).start()

    receive_main(1)
    raise_level(1)
    send_level(2)
    receive_rest(1)

    keep_p = jnp.where(core == 0, mask_ref[0, 3], mask_ref[0, 1])
    keep_f = jnp.where(core == 0, mask_ref[0, 1], mask_ref[0, 3])
    for copy in near_p:
        copy.wait_recv()
    near_tile(near_pts.at[0], near_chg.at[0], keep_p)
    forwarded(1).wait_recv()
    raise_rest(1)

    receive_main(2)
    raise_level(2)
    send_level(3)
    receive_rest(2)
    sibling_field(1)
    forwarded(2).wait_recv()
    raise_rest(2)
    sibling_field(2)

    receive_main(3)
    raise_level(3)
    send_level(4)
    receive_rest(3)

    near_a = [
        remote(pts_t, near_pts.at[1], 49, 19, (leaf + 2, grp)),
        remote(ordered, near_chg.at[1], 50, 20, (leaf + 2, grp)),
    ]
    near_b = [
        remote(pts_t, near_pts.at[2], 51, 21, (leaf - 2, grp)),
        remote(ordered, near_chg.at[2], 52, 22, (leaf - 2, grp)),
    ]

    @pl.when(has_b)
    def _():
        for copy in near_a:
            copy.start()

    @pl.when(has_a)
    def _():
        for copy in near_b:
            copy.start()

    forwarded(3).wait_recv()
    raise_rest(3)
    sibling_field(3)

    receive_main(4)
    raise_level(4)
    send_level(5)
    receive_rest(4)
    forwarded(4).wait_recv()
    raise_rest(4)
    sibling_field(4)

    receive_main(5)
    raise_level(5)

    message = pl.ds(COORD, TOP)
    top_copies = []
    for step in sorted(range(1, n_grp), key=lambda d: -min(d, n_grp - d)):
        copy = remote(
            own.at[LEVELS, core].at[message, :],
            top.at[step - 1, core],
            53 + step,
            23 + step,
            (leaf, (grp + step) % n_grp),
        )
        copy.start()
        top_copies.append((step, copy))

    receive_rest(5)
    forwarded(5).wait_recv()
    raise_rest(5)
    sibling_field(5)

    pass_on_a = [
        remote(near_pts.at[1], near_pts.at[3], 68, 38, partner),
        remote(near_chg.at[1], near_chg.at[3], 69, 39, partner),
    ]
    pass_on_b = [
        remote(near_pts.at[2], near_pts.at[3], 68, 38, partner),
        remote(near_chg.at[2], near_chg.at[3], 69, 39, partner),
    ]

    @pl.when(has_a)
    def _():
        for copy in near_a:
            copy.wait_recv()

        @pl.when(core == 1)
        def _():
            for copy in pass_on_a:
                copy.start()

    @pl.when(has_b)
    def _():
        for copy in near_b:
            copy.wait_recv()

        @pl.when(core == 0)
        def _():
            for copy in pass_on_b:
                copy.start()

    def top_forward(step, half):
        return remote(
            top.at[step - 1, half], top.at[step - 1, half], 60 + step, 30 + step, partner
        )

    @pl.when(has_a)
    def _():
        near_tile(near_pts.at[1], near_chg.at[1], mask_ref[0, 0])

    for step, copy in reversed(top_copies):
        copy.wait_recv()
        top_forward(step, core).start()

    @pl.when(has_b)
    def _():
        near_tile(near_pts.at[2], near_chg.at[2], mask_ref[0, 4])

    has_f = jnp.logical_or(
        jnp.logical_and(core == 0, has_a), jnp.logical_and(core == 1, has_b)
    )

    @pl.when(has_f)
    def _():
        for copy in pass_on_a:
            copy.wait_recv()
        near_tile(near_pts.at[3], near_chg.at[3], keep_f)

    target = jnp.concatenate(
        [own[LEVELS, 0, COORD:WEIGHT, :], own[LEVELS, 1, COORD:WEIGHT, :]], axis=0
    )
    potential = jnp.zeros((RHS, SK), F32)
    for step, _ in reversed(top_copies):
        top_forward(step, other).wait_recv()
        source = jnp.concatenate([top[step - 1, half, 0:HALF_DIM, :] for half in range(2)], axis=0)
        kern_high, kern_low = split(pair_kernel(jnp.transpose(source), target))
        high = jnp.concatenate(
            [top[step - 1, half, HALF_DIM:TOP, :] for half in range(2)], axis=0
        )
        potential = potential + dot(high, kern_high) + dot(high, kern_low)

    def times(value, matrix):
        high, low = split(value)
        both = dot(jnp.concatenate([high, low], axis=0), matrix)
        return both[:RHS] + both[RHS:]

    for level in range(LEVELS - 1, -1, -1):
        potential = times(potential, transfer[level]) + far[level]
    out_ref[...] = near[...] + times(potential, interp[...])

    first.wait_send()
    for copy in near_p:
        copy.wait_send()
    for level in routes:
        finish_sends(level)
        forward(level).wait_send()

    @pl.when(has_b)
    def _():
        for copy in near_a:
            copy.wait_send()

        @pl.when(core == 0)
        def _():
            for copy in pass_on_b:
                copy.wait_send()

    @pl.when(has_a)
    def _():
        for copy in near_b:
            copy.wait_send()

        @pl.when(core == 1)
        def _():
            for copy in pass_on_a:
                copy.wait_send()

    for step, copy in top_copies:
        copy.wait_send()
        top_forward(step, core).wait_send()


def solution(mesh):
    n_grp = mesh.shape["grp"]
    n_x, n_y = 4, mesh.shape["leaf"] // 8
    vmem = pltpu.VMEM

    def local(points, charges, order, near_mask, skeletons, leaf_interp, transfer):
        anywhere = pl.BlockSpec(memory_space=pl.ANY)
        return pl.pallas_call(
            functools.partial(kernel, n_y, n_x, n_grp),
            out_shape=jax.ShapeDtypeStruct((RHS, LEAF), F32),
            in_specs=[anywhere] * 3 + [pl.BlockSpec(memory_space=pltpu.SMEM)] + [anywhere] * 3,
            out_specs=pl.BlockSpec(memory_space=pltpu.VMEM),
            scratch_shapes=[
                vmem((DIM, LEAF), BF16),
                vmem((RHS, LEAF), BF16),
                vmem((1, LEAF), jnp.int32),
                vmem((LEVELS + 1, SK), jnp.int32),
                vmem((SK, LEAF), BF16),
                vmem((LEVELS, SK, SK), BF16),
                vmem((LEAF, DIM), BF16),
                vmem((RHS, LEAF), BF16),
                vmem((1, LEAF), F32),
                vmem((4, LEAF, DIM), BF16),
                vmem((4, RHS, LEAF), BF16),
                vmem((RHS, LEAF), F32),
                vmem((LEVELS + 1, 2, BUNDLE, SK), BF16),
                vmem((LEVELS, 2, BUNDLE, SK), BF16),
                vmem((n_grp - 1, 2, TOP, SK), BF16),
                vmem((LEVELS, RHS, SK), F32),
                pltpu.SemaphoreType.DMA((6,)),
                pltpu.SemaphoreType.DMA((70,)),
                pltpu.SemaphoreType.DMA((40,)),
            ],
            compiler_params=pltpu.CompilerParams(
                collective_id=0, has_side_effects=True, vmem_limit_bytes=48 * 1024 * 1024
            ),
        )(
            points,
            charges,
            order.reshape(1, LEAF),
            near_mask,
            skeletons.reshape(LEVELS + 1, SK),
            leaf_interp,
            transfer.reshape(LEVELS, SK, SK),
        )

    in_specs = (
        P(None, ("leaf", "grp")),
        P(None, ("leaf", "grp")),
        P(("leaf", "grp")),
        P(("leaf", "grp"), None),
        P(("leaf", "grp"), None, None),
        P(None, ("leaf", "grp")),
        P(("leaf", "grp"), None, None, None),
    )
    out_specs = P(None, ("leaf", "grp"))
    return jax.shard_map(local, mesh=mesh, in_specs=in_specs, out_specs=out_specs, check_vma=False)
```

time: 150 us -> 68.5 us (0.46)
  the two profiles are of different devices: /device:TPU:16 before, /device:TPU:3 now
where the time goes in v1:
time: 68.5 us; the launch traced here: 68.2 us
  Pallas kernels  62.3 us (91%)
  local copies, waits for them, and re-layouts  5.9 us (9%)
    pallas_call x1, Pallas kernels, local(): pl.pallas_call(functools.partial(kernel, n_y, n_x, n_grp), out_shape=jax....  62.3 us
    unnamed x16, local copies, waits for them, and re-layouts  5.9 us

profile of v1, /device:TPU:3, one launch (start us, length us, event | category | flops | bytes accessed | tf_op | source)
XLA Modules:
  0.0 68.2 jit_solution(8319454447022700711)
XLA Ops:
  0.0 0.0 copy-start.6
  0.0 0.7 %copy-done.6 = s32[1,7,128]{2,0,1:T(1,128)S(1)} copy-done((s32[1,7,128]{2,0,1:T(1,128)S(1)}, s32[1,7,128]{2,0,1:T(1,128)}, u32[]{:S(2)}) %copy-start.6) | copy-done | bytes 3608
  0.7 0.0 copy-start.4
  0.7 0.0 copy-start.5
  0.7 0.7 copy-done.4
  1.4 0.0 copy-done.5
  1.4 0.0 copy-start
  1.4 1.0 %copy-done = bf16[256,1024]{1,0:T(8,128)(2,1)S(1)} copy-done((bf16[256,1024]{1,0:T(8,128)(2,1)S(1)}, bf16[256,1024]{1,0:T(8,128)(2,1)}, u32[]{:S(2)}) %copy-start) | copy-done | bytes 524312
  2.4 0.0 copy-start.1
  2.4 0.9 %copy-done.1 = bf16[128,1024]{1,0:T(8,128)(2,1)S(1)} copy-done((bf16[128,1024]{1,0:T(8,128)(2,1)S(1)}, bf16[128,1024]{1,0:T(8,128)(2,1)}, u32[]{:S(2)}) %copy-start.1) | copy-done | bytes 262168
  3.4 0.0 copy-start.2
  3.4 0.9 %copy-done.2 = bf16[1,6,128,128]{3,2,1,0:T(8,128)(2,1)S(1)} copy-done((bf16[1,6,128,128]{3,2,1,0:T(8,128)(2,1)S(1)}, bf16[1,6,128,128]{3,2,1,0:T(8,128)(2,1)}, u32[]{:S(2)}) %copy-start.2) | copy-done | bytes 196632
  4.3 0.0 copy-start.3
  4.3 0.9 %copy-done.3 = bf16[64,1024]{1,0:T(8,128)(2,1)S(1)} copy-done((bf16[64,1024]{1,0:T(8,128)(2,1)S(1)}, bf16[64,1024]{1,0:T(8,128)(2,1)}, u32[]{:S(2)}) %copy-start.3) | copy-done | bytes 131096
  5.2 62.3 %shard_map.73 = f32[64,1024]{1,0:T(8,128)S(1)} custom-call(bf16[256,1024]{1,0:T(8,128)(2,1)S(1)} %copy-done, bf16[64,1024]{1,0:T(8,128)(2,1)S(1)} %copy-done.3, s32[1,1024]{1,0:T(1,128)S(1)} %bitcast.7, s32[1,5]{1,0:T(1,128)S(1)} %copy-done.5, s32[7,128]{1,0:T(8,128)S(1)} %bitcast.6, bf16[128,1024]{1,0:T(8,128)(2,1)S(1)} %copy-done.1, ...), custom_call_target="tpu_custom_call" | custom-call | tf_op jit(solution)/shard_map/pallas_call | solution.py:541
  67.5 0.7 %copy.12 = f32[64,1024]{1,0:T(8,128)} copy(f32[64,1024]{1,0:T(8,128)S(1)} %shard_map.73) | data formatting | bytes 524288
  (1 shorter events, 0.0 us)
Async XLA Ops:
  0.0 0.7 %copy-start.6 = (s32[1,7,128]{2,0,1:T(1,128)S(1)}, s32[1,7,128]{2,0,1:T(1,128)}, u32[]{:S(2)}) copy-start(s32[1,7,128]{2,0,1:T(1,128)} %param.11) | copy-start | bytes 10756
  0.7 0.7 %copy-start.4 = (s32[1024]{0:T(1024)S(1)}, s32[1024]{0:T(1024)}, u32[]{:S(2)}) copy-start(s32[1024]{0:T(1024)} %param.9) | copy-start | bytes 12292
  0.7 0.7 %copy-start.5 = (s32[1,5]{1,0:T(1,128)S(1)}, s32[1,5]{1,0:T(1,128)}, u32[]{:S(2)}) copy-start(s32[1,5]{1,0:T(1,128)} %mask_ref.1) | copy-start | bytes 64
  1.4 1.0 %copy-start = (bf16[256,1024]{1,0:T(8,128)(2,1)S(1)}, bf16[256,1024]{1,0:T(8,128)(2,1)}, u32[]{:S(2)}) copy-start(bf16[256,1024]{1,0:T(8,128)(2,1)} %points_hbm.1) | copy-start | bytes 1572868
  2.4 0.9 %copy-start.1 = (bf16[128,1024]{1,0:T(8,128)(2,1)S(1)}, bf16[128,1024]{1,0:T(8,128)(2,1)}, u32[]{:S(2)}) copy-start(bf16[128,1024]{1,0:T(8,128)(2,1)} %interp_hbm.1) | copy-start | bytes 786436
  3.4 0.9 %copy-start.2 = (bf16[1,6,128,128]{3,2,1,0:T(8,128)(2,1)S(1)}, bf16[1,6,128,128]{3,2,1,0:T(8,128)(2,1)}, u32[]{:S(2)}) copy-start(bf16[1,6,128,128]{3,2,1,0:T(8,128)(2,1)} %param.13) | copy-start | bytes 589828
  4.3 0.9 %copy-start.3 = (bf16[64,1024]{1,0:T(8,128)(2,1)S(1)}, bf16[64,1024]{1,0:T(8,128)(2,1)}, u32[]{:S(2)}) copy-start(bf16[64,1024]{1,0:T(8,128)(2,1)} %charges_hbm.1) | copy-start | bytes 393220

commit v2 on v1

--- a/solution.py
+++ b/solution.py
@@ -17,6 +17,7 @@
 TOP = HALF_DIM + HALF_RHS
 SCALE = 2.0 / DIM / math.log(2.0)
 CHUNK = 256
+N_PIECE = 10
 
 
 def dot(a, b):
@@ -128,7 +129,7 @@
     loads[3].wait()
     loads[4].wait()
     rows = lax.broadcasted_iota(jnp.int32, (LEAF, SK), 0)
-    pick = jnp.where(rows == skel[0:1, :], 1.0, 0.0).astype(BF16)
+    pick = jnp.where(rows == skel[0], 1.0, 0.0).astype(BF16)
     coords = dot(pts[...], pick).astype(BF16)
     loads[5].wait()
 
@@ -184,7 +185,7 @@
     bits = [core, y % 2, (y // 2) % 2, (y // 4) % 2, x % 2, (x // 2) % 2]
 
     def selection(level):
-        wanted = skel[level + 1 : level + 2, :]
+        wanted = skel[level + 1]
         rows = lax.broadcasted_iota(jnp.int32, (SK, SK), 0)
         upper = bits[level] * SK
         mine = jnp.where(rows + upper == wanted, 1.0, 0.0).astype(BF16)
@@ -319,48 +320,106 @@
             partner,
         )
 
+    sent = []
+    due = {}
+
+    def start(copy, condition=None):
+        when(condition, copy.start)
+        sent.append((condition, copy))
+
+    def expect(name, copy, condition=None):
+        due[name] = (condition, copy)
+
+    def arrive(name):
+        condition, copy = due.pop(name)
+        when(condition, copy.wait_recv)
+
+    def finish():
+        for name in list(due):
+            arrive(name)
+        for condition, copy in sent:
+            when(condition, copy.wait_send)
+
     def send_level(level):
         for condition, copy in copies[level][0] + copies[level][1]:
-            when(condition, copy.start)
-
-    def finish_sends(level):
-        for condition, copy in copies[level][0] + copies[level][1]:
-            when(condition, copy.wait_send)
-
-    first.wait_recv()
+            start(copy, condition)
+        expect(("main", level), copies[level][0][0][1])
+        expect(("rest", level), copies[level][1][0][1])
+
+    def receive_main(level):
+        arrive(("main", level))
+
+    def receive_rest(level):
+        arrive(("rest", level))
+        start(forward(level))
+        expect(("forward", level), forwarded(level))
+
+    piece_rows = LEAF // (N_PIECE - 2)
+    near_a, near_b = [], []
+    for slot, shift, there, group in ((1, 2, has_b, near_a), (2, -2, has_a, near_b)):
+        for index in range(N_PIECE):
+            if index < 2:
+                part = pl.ds(index * (RHS // 2), RHS // 2)
+                source, target = ordered.at[part, :], near_chg.at[slot, part, :]
+            else:
+                part = pl.ds((index - 2) * piece_rows, piece_rows)
+                source, target = pts_t.at[part, :], near_pts.at[slot, part, :]
+            group.append(
+                remote(
+                    source,
+                    target,
+                    70 + (slot - 1) * N_PIECE + index,
+                    40 + (slot - 1) * N_PIECE + index,
+                    (leaf + shift, grp),
+                )
+            )
+    pieces_sent = []
+
+    def send_pieces(count):
+        for _ in range(count):
+            index = len(pieces_sent)
+            pieces_sent.append(index)
+            start(near_a[index], has_b)
+            start(near_b[index], has_a)
+            expect(("a", index), near_a[index], has_a)
+            expect(("b", index), near_b[index], has_b)
+
+    sent.append((None, first))
+    sent.extend((None, copy) for copy in near_p)
+    expect("first", first)
+    expect("p0", near_p[0])
+    expect("p1", near_p[1])
+    send_pieces(2)
+    arrive("first")
     raise_level(0)
     send_level(1)
+    send_pieces(2)
     raise_rest(0)
     sibling_field(0)
 
     near_tile(pts_t, ordered, None)
-
-    def receive_main(level):
-        copies[level][0][0][1].wait_recv()
-
-    def receive_rest(level):
-        copies[level][1][0][1].wait_recv()
-        forward(level).start()
 
     receive_main(1)
     raise_level(1)
     send_level(2)
+    send_pieces(2)
     receive_rest(1)
 
     keep_p = jnp.where(core == 0, mask_ref[0, 3], mask_ref[0, 1])
     keep_f = jnp.where(core == 0, mask_ref[0, 1], mask_ref[0, 3])
-    for copy in near_p:
-        copy.wait_recv()
+    arrive("p0")
+    arrive("p1")
     near_tile(near_pts.at[0], near_chg.at[0], keep_p)
-    forwarded(1).wait_recv()
+    arrive(("forward", 1))
     raise_rest(1)
 
     receive_main(2)
     raise_level(2)
     send_level(3)
+    send_pieces(2)
     receive_rest(2)
     sibling_field(1)
-    forwarded(2).wait_recv()
+    arrive(("forward", 2))
     raise_rest(2)
     sibling_field(2)
 
@@ -369,26 +428,8 @@
     send_level(4)
     receive_rest(3)
 
-    near_a = [
-        remote(pts_t, near_pts.at[1], 49, 19, (leaf + 2, grp)),
-        remote(ordered, near_chg.at[1], 50, 20, (leaf + 2, grp)),
-    ]
-    near_b = [
-        remote(pts_t, near_pts.at[2], 51, 21, (leaf - 2, grp)),
-        remote(ordered, near_chg.at[2], 52, 22, (leaf - 2, grp)),
-    ]
-
-    @pl.when(has_b)
-    def _():
-        for copy in near_a:
-            copy.start()
-
-    @pl.when(has_a)
-    def _():
-        for copy in near_b:
-            copy.start()
-
-    forwarded(3).wait_recv()
+    send_pieces(2)
+    arrive(("forward", 3))
     raise_rest(3)
     sibling_field(3)
 
@@ -396,7 +437,7 @@
     raise_level(4)
     send_level(5)
     receive_rest(4)
-    forwarded(4).wait_recv()
+    arrive(("forward", 4))
     raise_rest(4)
     sibling_field(4)
 
@@ -413,11 +454,12 @@
             23 + step,
             (leaf, (grp + step) % n_grp),
         )
-        copy.start()
+        start(copy)
+        expect(("top", step), copy)
         top_copies.append((step, copy))
 
     receive_rest(5)
-    forwarded(5).wait_recv()
+    arrive(("forward", 5))
     raise_rest(5)
     sibling_field(5)
 
@@ -430,25 +472,16 @@
         remote(near_chg.at[2], near_chg.at[3], 69, 39, partner),
     ]
 
-    @pl.when(has_a)
-    def _():
-        for copy in near_a:
-            copy.wait_recv()
-
-        @pl.when(core == 1)
-        def _():
-            for copy in pass_on_a:
-                copy.start()
-
-    @pl.when(has_b)
-    def _():
-        for copy in near_b:
-            copy.wait_recv()
-
-        @pl.when(core == 0)
-        def _():
-            for copy in pass_on_b:
-                copy.start()
+    has_f = jnp.logical_or(
+        jnp.logical_and(core == 0, has_a), jnp.logical_and(core == 1, has_b)
+    )
+    for index in range(N_PIECE):
+        arrive(("a", index))
+        arrive(("b", index))
+    for index in range(2):
+        start(pass_on_a[index], jnp.logical_and(core == 1, has_a))
+        start(pass_on_b[index], jnp.logical_and(core == 0, has_b))
+        expect(("f", index), pass_on_a[index], has_f)
 
     def top_forward(step, half):
         return remote(
@@ -460,21 +493,19 @@
         near_tile(near_pts.at[1], near_chg.at[1], mask_ref[0, 0])
 
     for step, copy in reversed(top_copies):
-        copy.wait_recv()
-        top_forward(step, core).start()
+        arrive(("top", step))
+        start(top_forward(step, core))
+        expect(("top forward", step), top_forward(step, other))
 
     @pl.when(has_b)
     def _():
         near_tile(near_pts.at[2], near_chg.at[2], mask_ref[0, 4])
 
-    has_f = jnp.logical_or(
-        jnp.logical_and(core == 0, has_a), jnp.logical_and(core == 1, has_b)
-    )
+    arrive(("f", 0))
+    arrive(("f", 1))
 
     @pl.when(has_f)
     def _():
-        for copy in pass_on_a:
-            copy.wait_recv()
         near_tile(near_pts.at[3], near_chg.at[3], keep_f)
 
     target = jnp.concatenate(
@@ -482,7 +513,7 @@
     )
     potential = jnp.zeros((RHS, SK), F32)
     for step, _ in reversed(top_copies):
-        top_forward(step, other).wait_recv()
+        arrive(("top forward", step))
         source = jnp.concatenate([top[step - 1, half, 0:HALF_DIM, :] for half in range(2)], axis=0)
         kern_high, kern_low = split(pair_kernel(jnp.transpose(source), target))
         high = jnp.concatenate(
@@ -499,36 +530,7 @@
         potential = times(potential, transfer[level]) + far[level]
     out_ref[...] = near[...] + times(potential, interp[...])
 
-    first.wait_send()
-    for copy in near_p:
-        copy.wait_send()
-    for level in routes:
-        finish_sends(level)
-        forward(level).wait_send()
-
-    @pl.when(has_b)
-    def _():
-        for copy in near_a:
-            copy.wait_send()
-
-        @pl.when(core == 0)
-        def _():
-            for copy in pass_on_b:
-                copy.wait_send()
-
-    @pl.when(has_a)
-    def _():
-        for copy in near_b:
-            copy.wait_send()
-
-        @pl.when(core == 1)
-        def _():
-            for copy in pass_on_a:
-                copy.wait_send()
-
-    for step, copy in top_copies:
-        copy.wait_send()
-        top_forward(step, core).wait_send()
+    finish()
 
 
 def solution(mesh):
@@ -537,7 +539,7 @@
     vmem = pltpu.VMEM
 
     def local(points, charges, order, near_mask, skeletons, leaf_interp, transfer):
-        anywhere = pl.BlockSpec(memory_space=pl.ANY)
+        anywhere = pl.BlockSpec(memory_space=pltpu.HBM)
         return pl.pallas_call(
             functools.partial(kernel, n_y, n_x, n_grp),
             out_shape=jax.ShapeDtypeStruct((RHS, LEAF), F32),
@@ -547,7 +549,7 @@
                 vmem((DIM, LEAF), BF16),
                 vmem((RHS, LEAF), BF16),
                 vmem((1, LEAF), jnp.int32),
-                vmem((LEVELS + 1, SK), jnp.int32),
+                vmem((LEVELS + 1, 1, SK), jnp.int32),
                 vmem((SK, LEAF), BF16),
                 vmem((LEVELS, SK, SK), BF16),
                 vmem((LEAF, DIM), BF16),
@@ -561,18 +563,18 @@
                 vmem((n_grp - 1, 2, TOP, SK), BF16),
                 vmem((LEVELS, RHS, SK), F32),
                 pltpu.SemaphoreType.DMA((6,)),
-                pltpu.SemaphoreType.DMA((70,)),
-                pltpu.SemaphoreType.DMA((40,)),
+                pltpu.SemaphoreType.DMA((70 + 2 * N_PIECE,)),
+                pltpu.SemaphoreType.DMA((40 + 2 * N_PIECE,)),
             ],
             compiler_params=pltpu.CompilerParams(
-                collective_id=0, has_side_effects=True, vmem_limit_bytes=48 * 1024 * 1024
+                collective_id=0, has_side_effects=True, vmem_limit_bytes=67_043_328
             ),
         )(
             points,
             charges,
             order.reshape(1, LEAF),
             near_mask,
-            skeletons.reshape(LEVELS + 1, SK),
+            jnp.transpose(skeletons, (1, 0, 2)),
             leaf_interp,
             transfer.reshape(LEVELS, SK, SK),
         )

time: 68.5 us -> 57.4 us (0.84)
  the two profiles are of different devices: /device:TPU:3 before, /device:TPU:1 now
where the time goes in v2:
time: 57.4 us; the launch traced here: 56.3 us
  Pallas kernels  54.6 us (95%)
  local copies, waits for them, and re-layouts  1.67 us (3%)
    pallas_call x1, Pallas kernels, local(): pl.pallas_call(functools.partial(kernel, n_y, n_x, n_grp), out_shape=jax....  54.6 us
    unnamed x1, local copies, waits for them, and re-layouts  1.67 us

profile of v2, /device:TPU:1, one launch (start us, length us, event | category | flops | bytes accessed | tf_op | source)
XLA Modules:
  0.0 56.3 jit_solution(4121799105312222280)
XLA Ops:
  0.0 54.6 %shard_map.73 = f32[64,1024]{1,0:T(8,128)} custom-call(bf16[256,1024]{1,0:T(8,128)(2,1)} %points_hbm.1, bf16[64,1024]{1,0:T(8,128)(2,1)} %charges_hbm.1, s32[1,1024]{1,0:T(1,128)} %bitcast.4, s32[1,5]{1,0:T(1,128)} %mask_ref.1, s32[7,1,128]{2,1,0:T(1,128)} %bitcast.5, bf16[128,1024]{1,0:T(8,128)(2,1)} %interp_hbm.1, bf16[6,128,128]{2,1,0:T(8,128)(2,1)} %bitcast.3), custom_call_target="tpu_custom_call" | custom-call | tf_op jit(solution)/shard_map/pallas_call | solution.py:543
  54.6 1.7 %copy.9 = f32[64,1024]{1,0:T(8,128)} copy(f32[64,1024]{1,0:T(8,128)} %shard_map.73) | data formatting | bytes 524288

commit v3 on v0

v3 whole, which is shorter than its diff:
```python
import functools
import itertools
import math

import jax
import jax.numpy as jnp
from jax import lax
from jax.experimental import pallas as pl
from jax.experimental.pallas import tpu as pltpu
from jax.sharding import PartitionSpec as P

MESH = pl.DeviceIdType.MESH
F32 = jnp.float32
BF16 = jnp.bfloat16
DIM, RHS, SK, LEAF, LEVELS = 256, 64, 128, 1024, 6
PART_DIM, PART_RHS = DIM // 4, RHS // 4
COORD = 2 * PART_RHS
WEIGHT = COORD + PART_DIM
LOW = WEIGHT + PART_RHS
BUNDLE = LOW + PART_RHS
TOP = PART_DIM + PART_RHS
SCALE = 2.0 / DIM / math.log(2.0)
CHUNK = 256
N_PIECE = 10
PIECES = (2, 3, 3, 2, 0)


def dot(a, b):
    return jnp.dot(a, b, preferred_element_type=F32)


def dot_nt(a, b):
    return lax.dot_general(a, b, (((1,), (1,)), ((), ())), preferred_element_type=F32)


def split(value):
    high = value.astype(BF16)
    low = (value - high.astype(F32)).astype(BF16)
    return high, low


def pair_kernel(source_t, target):
    wide_s = source_t.astype(F32)
    wide_t = target.astype(F32)
    square_s = jnp.sum(wide_s * wide_s, axis=1, keepdims=True) * SCALE
    square_t = jnp.sum(wide_t * wide_t, axis=0, keepdims=True) * SCALE
    return jnp.exp2(dot(source_t, target) * (2.0 * SCALE) - (square_s + square_t))


def kernel(
    n_y, n_x, n_grp,
    points_hbm, charges_hbm, order_hbm, mask_ref, skel_hbm, interp_hbm, transfer_hbm,
    out_ref,
    pts, chg, order, skel, interp, transfer,
    pts_t, ordered, norm_t, near_pts, near_chg, near, back,
    coords, first, second, bundle, sib, cousin, top, far,
    load_sem, send_sem, recv_sem,
):
    leaf = lax.axis_index("leaf")
    grp = lax.axis_index("grp")
    core = leaf % 2
    other = 1 - core
    chip = leaf // 2
    y = chip % n_y
    x = chip // n_y
    odd = y % 2
    quarter = 2 * core + odd
    n_chip = n_x * n_y
    has_a = chip > 0
    has_b = chip < n_chip - 1

    def at_yx(yy, xx):
        return ((xx * n_y + (yy + n_y) % n_y) * 2 + core, grp)

    partner = (chip * 2 + other, grp)
    beside = at_yx(y + 1 - 2 * odd, x)
    across_x = (x + 2) % n_x
    family = {
        2: [
            at_yx(y + 2 - 4 * ((y // 2) % 2), x),
            at_yx(y - 2 + 4 * ((y // 2) % 2), x),
            at_yx(y + 4, x),
        ],
        4: [at_yx(y, x + 1 - 2 * (x % 2)), at_yx(y, n_x - 1 - x), at_yx(y, across_x)],
    }
    bits = [core, odd, (y // 2) % 2, (y // 4) % 2, x % 2, (x // 2) % 2]

    loads = [
        pltpu.make_async_copy(src, dst, load_sem.at[i])
        for i, (src, dst) in enumerate(
            [
                (order_hbm, order),
                (charges_hbm, chg),
                (interp_hbm, interp),
                (skel_hbm, skel),
                (points_hbm, pts),
                (transfer_hbm, transfer),
            ]
        )
    ]
    for load in loads:
        load.start()

    barrier = pltpu.get_barrier_semaphore()
    peers = [partner, beside] + family[2] + family[4] + [(leaf, (grp + step) % n_grp) for step in range(1, n_grp)]
    for peer in peers:
        pl.semaphore_signal(barrier, inc=1, device_id=peer, device_id_type=MESH)

    @pl.when(has_a)
    def _():
        pl.semaphore_signal(barrier, inc=1, device_id=(leaf - 2, grp), device_id_type=MESH)

    @pl.when(has_b)
    def _():
        pl.semaphore_signal(barrier, inc=1, device_id=(leaf + 2, grp), device_id_type=MESH)

    numbers = itertools.count()
    sent = []
    due = {}

    def remote(src, dst, send, recv, device):
        return pltpu.make_async_remote_copy(
            src_ref=src,
            dst_ref=dst,
            send_sem=send_sem.at[send],
            recv_sem=recv_sem.at[recv],
            device_id=device,
            device_id_type=MESH,
        )

    def when(condition, action):
        if condition is None:
            action()
        else:
            pl.when(condition)(action)

    def exchange(name, src, dst, arriving, device, send_if=None, due_if=None):
        number = next(numbers)
        copy = remote(src, dst, number, number, device)
        when(send_if, copy.start)
        sent.append((send_if, copy))
        due[name] = (due_if, remote(arriving, arriving, number, number, device))

    def arrive(name):
        condition, copy = due.pop(name)
        when(condition, copy.wait_recv)

    def finish():
        for name in list(due):
            arrive(name)
        for condition, copy in sent:
            when(condition, copy.wait_send)

    loads[0].wait()
    loads[1].wait()
    for column in range(0, LEAF, CHUNK):
        wanted = order[:, column : column + CHUNK]
        rows = lax.broadcasted_iota(jnp.int32, (LEAF, CHUNK), 0)
        pick = jnp.where(rows == wanted, 1.0, 0.0).astype(BF16)
        ordered[:, column : column + CHUNK] = dot(chg[...], pick).astype(BF16)
    loads[2].wait()
    weights = dot_nt(ordered[...], interp[...])
    loads[3].wait()
    loads[4].wait()
    rows = lax.broadcasted_iota(jnp.int32, (LEAF, SK), 0)
    pick = jnp.where(rows == skel[0], 1.0, 0.0).astype(BF16)
    coords[0] = dot(pts[...], pick).astype(BF16)
    loads[5].wait()

    def contribution(weights, level):
        high, low = split(weights)
        both = dot_nt(jnp.concatenate([high, low], axis=0), transfer[level])
        count = weights.shape[0]
        contrib = both[:count] + both[count:]
        return (*split(contrib), high, low), contrib

    def put(ref, index, values, rows):
        contrib_high, contrib_low, high, low = (v[rows] for v in values)
        ref[index, 0:PART_RHS] = contrib_high
        ref[index, PART_RHS:COORD] = contrib_low
        ref[index, WEIGHT:LOW] = high
        ref[index, LOW:BUNDLE] = low

    values, _ = contribution(weights, 0)
    for index in range(4):
        put(first, index, values, slice(index * PART_RHS, (index + 1) * PART_RHS))
        first[index, COORD:WEIGHT] = coords[0, index * PART_DIM : (index + 1) * PART_DIM]

    expected = len(peers) + has_a.astype(jnp.int32) + has_b.astype(jnp.int32)
    pl.semaphore_wait(barrier, expected)

    mine, theirs = pl.ds(2 * core, 2), pl.ds(2 * other, 2)
    exchange("first", first.at[theirs], sib.at[0, theirs], sib.at[0, mine], partner)
    exchange("first rest", first.at[mine], sib.at[0, mine], sib.at[0, theirs], partner)
    for row in range(0, LEAF, CHUNK):
        pts_t[row : row + CHUNK, :] = jnp.transpose(pts[:, row : row + CHUNK])
    exchange("p0", pts_t, near_pts.at[0], near_pts.at[0], partner)
    exchange("p1", ordered, near_chg.at[0], near_chg.at[0], partner)

    forth = 4 * core - 2
    onward, backward = (leaf + forth, grp), (leaf - forth, grp)
    to_there = jnp.where(core == 1, has_b, has_a)
    from_there = jnp.where(core == 1, has_a, has_b)
    piece_rows = LEAF // (N_PIECE - 2)
    pieces = iter(range(N_PIECE))

    def send_pieces(count):
        for index in itertools.islice(pieces, count):
            if index < 2:
                part = pl.ds(index * (RHS // 2), RHS // 2)
                source, target = ordered.at[part, :], near_chg.at[1, part, :]
            else:
                part = pl.ds((index - 2) * piece_rows, piece_rows)
                source, target = pts_t.at[part, :], near_pts.at[1, part, :]
            exchange(("near", index), source, target, target, onward, to_there, from_there)

    send_pieces(PIECES[0])
    wide = pts[...].astype(F32)
    norm_t[...] = jnp.sum(wide * wide, axis=0, keepdims=True) * SCALE
    near[...] = jnp.zeros_like(near)

    def near_tile(source_t, source_chg, keep, mirror=None):
        def body(step, carry):
            rows = pl.ds(pl.multiple_of(step * CHUNK, CHUNK), CHUNK)
            lhs = source_t[rows, :]
            wide = lhs.astype(F32)
            norm_s = jnp.sum(wide * wide, axis=1, keepdims=True) * SCALE
            charge = source_chg[:, rows]
            if keep is not None:
                charge = jnp.where(keep > 0, charge, jnp.zeros_like(charge))
            inner = dot(lhs, pts[...])
            tile = jnp.exp2(inner * (2.0 * SCALE) - (norm_s + norm_t[...])).astype(BF16)
            near[...] += dot(charge, tile)
            if mirror is not None:
                mirror[:, rows] = dot_nt(ordered[...], tile)
            return carry

        lax.fori_loop(0, LEAF // CHUNK, body, 0)

    def selection(level):
        wanted = skel[level + 1]
        rows = lax.broadcasted_iota(jnp.int32, (SK, SK), 0)
        upper = bits[level] * SK
        own = jnp.where(rows + upper == wanted, 1.0, 0.0).astype(BF16)
        far = jnp.where(rows + (SK - upper) == wanted, 1.0, 0.0).astype(BF16)
        return own, far

    def sib_coords(level):
        return jnp.concatenate([sib[level, q, COORD:WEIGHT, :] for q in range(4)], axis=0)

    def raise_part(level, own, there):
        pick_own, pick_far = selection(level)
        joined = dot(own[COORD:WEIGHT], pick_own) + dot(there[COORD:WEIGHT], pick_far)
        terms = [
            bundle_[rows].astype(F32)
            for bundle_ in (own, there)
            for rows in (slice(0, PART_RHS), slice(PART_RHS, COORD))
        ]
        return joined.astype(BF16), (terms[0] + terms[1]) + (terms[2] + terms[3])

    def raise_rest(level):
        own, far = selection(level)
        coords[level + 1] = (dot(coords[level], own) + dot(sib_coords(level), far)).astype(BF16)

    def sibling_field(level):
        source = jnp.transpose(sib_coords(level))
        kern_high, kern_low = split(pair_kernel(source, coords[level]))
        high = jnp.concatenate([sib[level, q, WEIGHT:LOW, :] for q in range(4)], axis=0)
        low = jnp.concatenate([sib[level, q, LOW:BUNDLE, :] for q in range(4)], axis=0)
        both = dot(jnp.concatenate([high, low], axis=0), kern_high)
        far[level] = both[:RHS] + both[RHS:] + dot(high, kern_low)

    lead = pl.ds(0, WEIGHT)
    tail = pl.ds(WEIGHT, BUNDLE - WEIGHT)
    body_rows = pl.ds(COORD, BUNDLE - COORD)

    def raise_first():
        results = [
            raise_part(0, first[2 * core + p], sib[0, 2 * core + p]) for p in range(2)
        ]
        values = contribution(jnp.concatenate([w for _, w in results], axis=0), 1)
        values = values[0]
        for p in range(2):
            put(second, p, values, slice(p * PART_RHS, (p + 1) * PART_RHS))
            second[p, COORD:WEIGHT] = results[p][0]

    def send_first():
        there, here = 2 * core + 1 - odd, 2 * core + odd
        exchange(
            ("main", 1), second.at[1 - odd, lead, :], sib.at[1, there, lead, :],
            sib.at[1, here, lead, :], beside,
        )
        exchange(
            ("tail", 1), second.at[1 - odd, tail, :], sib.at[1, there, tail, :],
            sib.at[1, here, tail, :], beside,
        )
        exchange(
            ("more", 1), second.at[odd, body_rows, :], sib.at[1, here, body_rows, :],
            sib.at[1, there, body_rows, :], beside,
        )

    def send_family(level, joined, weights):
        values, contrib = contribution(weights, level)
        put(bundle, level, values, slice(None))
        bundle[level, COORD:WEIGHT] = joined
        parent_values, _ = contribution(contrib, level + 1)
        put(bundle, level + 1, parent_values, slice(None))
        pick_own, _ = selection(level)
        bundle[level + 1, COORD:WEIGHT] = dot(joined, pick_own).astype(BF16)
        landing = sib.at[level, quarter]
        exchange(("sib", level), bundle.at[level], landing, landing, family[level][0])
        for index in range(2):
            landing = cousin.at[level // 4 * 2 + index]
            exchange(
                ("cousin", level, index), bundle.at[level + 1], landing, landing,
                family[level][1 + index],
            )

    def raise_family(level):
        arrive(("sib", level))
        joined, weights = raise_part(level, bundle[level], sib[level, quarter])
        _, contrib = contribution(weights, level + 1)
        own_pick, far_pick = selection(level + 1)
        arrive(("cousin", level, 0))
        arrive(("cousin", level, 1))
        parts = [cousin[level // 4 * 2 + index] for index in range(2)]
        coords_far = (
            parts[0][COORD:WEIGHT].astype(F32) + parts[1][COORD:WEIGHT].astype(F32)
        ).astype(BF16)
        above = (dot(joined, own_pick) + dot(coords_far, far_pick)).astype(BF16)
        contrib_far = sum_rows(parts, 0)
        return above, contrib + contrib_far, coords_far

    def sum_rows(parts, row):
        terms = [
            part[slice(row + shift, row + shift + PART_RHS)].astype(F32)
            for part in parts
            for shift in (0, PART_RHS)
        ]
        return (terms[0] + terms[1]) + (terms[2] + terms[3])

    def keep_cousins(level, coords_far):
        parts = [cousin[level // 4 * 2 + index] for index in range(2)]
        high, low = split(sum_rows(parts, WEIGHT))
        sib[level + 1, quarter, COORD:WEIGHT] = coords_far
        sib[level + 1, quarter, WEIGHT:LOW] = high
        sib[level + 1, quarter, LOW:BUNDLE] = low

    diagonal = 2 * core + 1 - odd
    across = 2 * other + odd
    corner = 2 * other + 1 - odd

    def spread(level):
        if level == 1:
            arrive(("tail", 1))
            arrive(("more", 1))
            exchange(
                ("core", level), sib.at[1, mine, body_rows, :], sib.at[1, mine, body_rows, :],
                sib.at[1, theirs, body_rows, :], partner,
            )
            return
        source = sib.at[level, quarter, body_rows, :]
        exchange(("core", level), source, source, sib.at[level, across, body_rows, :], partner)
        exchange(("side", level), source, source, sib.at[level, diagonal, body_rows, :], beside)

    def spread_side(level):
        arrive(("side", level))
        source = sib.at[level, diagonal, body_rows, :]
        exchange(("corner", level), source, source, sib.at[level, corner, body_rows, :], partner)

    def complete(level):
        arrive(("core", level))
        if level > 1:
            arrive(("corner", level))
        raise_rest(level)
        sibling_field(level)

    keep_p = jnp.where(core == 0, mask_ref[0, 3], mask_ref[0, 1])
    keep_f = jnp.where(core == 0, mask_ref[0, 1], mask_ref[0, 3])
    keep_in = jnp.where(core == 0, mask_ref[0, 4], mask_ref[0, 0])
    keep_out = jnp.where(core == 0, mask_ref[0, 0], mask_ref[0, 4])

    arrive("first")
    raise_first()
    send_first()
    send_pieces(PIECES[1])
    arrive("first rest")
    raise_rest(0)
    sibling_field(0)

    arrive(("main", 1))
    joined, weights = raise_part(1, second[odd], sib[1, quarter, 0:WEIGHT])
    send_family(2, joined, weights)
    send_pieces(PIECES[2])
    spread(1)
    near_tile(pts_t, ordered, None)
    complete(1)

    joined, weights, coords_far = raise_family(2)
    send_family(4, joined, weights)
    send_pieces(PIECES[3])
    keep_cousins(2, coords_far)
    spread(2)
    spread(3)
    for index in range(N_PIECE):
        arrive(("near", index))
    for name, ref in (("f0", near_pts), ("f1", near_chg)):
        exchange(name, ref.at[1], ref.at[2], ref.at[2], partner, from_there, to_there)

    @pl.when(from_there)
    def _():
        near_tile(near_pts.at[1], near_chg.at[1], keep_in, back.at[0])

    exchange("back", back.at[0], back.at[1], back.at[1], backward, from_there, to_there)

    joined, weights, coords_far = raise_family(4)
    bundle[LEVELS, COORD:WEIGHT] = joined
    bundle[LEVELS, WEIGHT:LOW] = weights.astype(BF16)

    steps = sorted(range(1, n_grp), key=lambda d: -min(d, n_grp - d))
    for step in steps:
        landing = top.at[step - 1, quarter]
        exchange(
            ("top", step), bundle.at[LEVELS, pl.ds(COORD, TOP), :], landing, landing,
            (leaf, (grp + step) % n_grp),
        )
    send_pieces(PIECES[4])
    keep_cousins(4, coords_far)
    spread(4)
    spread(5)
    spread_side(2)
    spread_side(3)
    arrive("p0")
    arrive("p1")
    near_tile(near_pts.at[0], near_chg.at[0], keep_p)
    complete(2)
    complete(3)

    def top_spread(step):
        arrive(("top", step))
        source = top.at[step - 1, quarter]
        exchange(("top core", step), source, source, top.at[step - 1, across], partner)
        exchange(("top side", step), source, source, top.at[step - 1, diagonal], beside)

    def top_spread_side(step):
        arrive(("top side", step))
        source = top.at[step - 1, diagonal]
        exchange(("top corner", step), source, source, top.at[step - 1, corner], partner)

    arrive("f0")
    arrive("f1")

    @pl.when(to_there)
    def _():
        near_tile(near_pts.at[2], near_chg.at[2], keep_f)

    for step in steps:
        top_spread(step)
    spread_side(4)
    spread_side(5)
    arrive("back")

    @pl.when(to_there)
    def _():
        near[...] += jnp.where(keep_out > 0, back[1], 0.0)

    for step in steps:
        top_spread_side(step)
    complete(4)
    complete(5)
    potential = jnp.zeros((RHS, SK), F32)
    for step in steps:
        arrive(("top core", step))
        arrive(("top corner", step))
        source = jnp.concatenate([top[step - 1, q, 0:PART_DIM, :] for q in range(4)], axis=0)
        kern_high, kern_low = split(pair_kernel(jnp.transpose(source), coords[LEVELS]))
        high = jnp.concatenate([top[step - 1, q, PART_DIM:TOP, :] for q in range(4)], axis=0)
        potential = potential + dot(high, kern_high) + dot(high, kern_low)

    def times(value, matrix):
        high, low = split(value)
        both = dot(jnp.concatenate([high, low], axis=0), matrix)
        return both[:RHS] + both[RHS:]

    for level in range(LEVELS - 1, -1, -1):
        potential = times(potential, transfer[level]) + far[level]
    out_ref[...] = near[...] + times(potential, interp[...])
    finish()


def solution(mesh):
    n_grp = mesh.shape["grp"]
    n_x, n_y = 4, mesh.shape["leaf"] // 8
    vmem = pltpu.VMEM

    def local(points, charges, order, near_mask, skeletons, leaf_interp, transfer):
        anywhere = pl.BlockSpec(memory_space=pltpu.HBM)
        return pl.pallas_call(
            functools.partial(kernel, n_y, n_x, n_grp),
            out_shape=jax.ShapeDtypeStruct((RHS, LEAF), F32),
            in_specs=[anywhere] * 3 + [pl.BlockSpec(memory_space=pltpu.SMEM)] + [anywhere] * 3,
            out_specs=pl.BlockSpec(memory_space=pltpu.VMEM),
            scratch_shapes=[
                vmem((DIM, LEAF), BF16),
                vmem((RHS, LEAF), BF16),
                vmem((1, LEAF), jnp.int32),
                vmem((LEVELS + 1, 1, SK), jnp.int32),
                vmem((SK, LEAF), BF16),
                vmem((LEVELS, SK, SK), BF16),
                vmem((LEAF, DIM), BF16),
                vmem((RHS, LEAF), BF16),
                vmem((1, LEAF), F32),
                vmem((3, LEAF, DIM), BF16),
                vmem((3, RHS, LEAF), BF16),
                vmem((RHS, LEAF), F32),
                vmem((2, RHS, LEAF), F32),
                vmem((LEVELS + 1, DIM, SK), BF16),
                vmem((4, BUNDLE, SK), BF16),
                vmem((2, BUNDLE, SK), BF16),
                vmem((LEVELS + 1, BUNDLE, SK), BF16),
                vmem((LEVELS, 4, BUNDLE, SK), BF16),
                vmem((4, BUNDLE, SK), BF16),
                vmem((n_grp - 1, 4, TOP, SK), BF16),
                vmem((LEVELS, RHS, SK), F32),
                pltpu.SemaphoreType.DMA((6,)),
                pltpu.SemaphoreType.DMA((96,)),
                pltpu.SemaphoreType.DMA((96,)),
            ],
            compiler_params=pltpu.CompilerParams(
                collective_id=0, has_side_effects=True, vmem_limit_bytes=67_043_328
            ),
        )(
            points,
            charges,
            order.reshape(1, LEAF),
            near_mask,
            jnp.transpose(skeletons, (1, 0, 2)),
            leaf_interp,
            transfer.reshape(LEVELS, SK, SK),
        )

    in_specs = (
        P(None, ("leaf", "grp")),
        P(None, ("leaf", "grp")),
        P(("leaf", "grp")),
        P(("leaf", "grp"), None),
        P(("leaf", "grp"), None, None),
        P(None, ("leaf", "grp")),
        P(("leaf", "grp"), None, None, None),
    )
    out_specs = P(None, ("leaf", "grp"))
    return jax.shard_map(local, mesh=mesh, in_specs=in_specs, out_specs=out_specs, check_vma=False)
```

time: 150 us -> 50 us (0.33)
  the two profiles are of different devices: /device:TPU:16 before, /device:TPU:1 now
where the time goes in v3:
time: 50 us; the launch traced here: 49.4 us
  Pallas kernels  47.7 us (95%)
  local copies, waits for them, and re-layouts  1.67 us (3%)
    pallas_call x1, Pallas kernels, local(): pl.pallas_call(functools.partial(kernel, n_y, n_x, n_grp), out_shape=jax....  47.7 us
    unnamed x1, local copies, waits for them, and re-layouts  1.67 us

profile of v3, /device:TPU:1, one launch (start us, length us, event | category | flops | bytes accessed | tf_op | source)
XLA Modules:
  0.0 49.4 jit_solution(2001629538325956260)
XLA Ops:
  0.0 47.7 %shard_map.73 = f32[64,1024]{1,0:T(8,128)} custom-call(bf16[256,1024]{1,0:T(8,128)(2,1)} %points_hbm.1, bf16[64,1024]{1,0:T(8,128)(2,1)} %charges_hbm.1, s32[1,1024]{1,0:T(1,128)} %bitcast.4, s32[1,5]{1,0:T(1,128)} %mask_ref.1, s32[7,1,128]{2,1,0:T(1,128)} %bitcast.5, bf16[128,1024]{1,0:T(8,128)(2,1)} %interp_hbm.1, bf16[6,128,128]{2,1,0:T(8,128)(2,1)} %bitcast.3), custom_call_target="tpu_custom_call" | custom-call | tf_op jit(solution)/shard_map/pallas_call | solution.py:498
  47.7 1.7 %copy.9 = f32[64,1024]{1,0:T(8,128)} copy(f32[64,1024]{1,0:T(8,128)} %shard_map.73) | data formatting | bytes 524288

commit v4 on v3

--- a/solution.py
+++ b/solution.py
@@ -22,7 +22,7 @@
 SCALE = 2.0 / DIM / math.log(2.0)
 CHUNK = 256
 N_PIECE = 10
-PIECES = (2, 3, 3, 2, 0)
+PIECES = (2, 2, 3, 3, 0)
 
 
 def dot(a, b):
@@ -192,10 +192,6 @@
     mine, theirs = pl.ds(2 * core, 2), pl.ds(2 * other, 2)
     exchange("first", first.at[theirs], sib.at[0, theirs], sib.at[0, mine], partner)
     exchange("first rest", first.at[mine], sib.at[0, mine], sib.at[0, theirs], partner)
-    for row in range(0, LEAF, CHUNK):
-        pts_t[row : row + CHUNK, :] = jnp.transpose(pts[:, row : row + CHUNK])
-    exchange("p0", pts_t, near_pts.at[0], near_pts.at[0], partner)
-    exchange("p1", ordered, near_chg.at[0], near_chg.at[0], partner)
 
     forth = 4 * core - 2
     onward, backward = (leaf + forth, grp), (leaf - forth, grp)
@@ -214,10 +210,6 @@
                 source, target = pts_t.at[part, :], near_pts.at[1, part, :]
             exchange(("near", index), source, target, target, onward, to_there, from_there)
 
-    send_pieces(PIECES[0])
-    wide = pts[...].astype(F32)
-    norm_t[...] = jnp.sum(wide * wide, axis=0, keepdims=True) * SCALE
-    near[...] = jnp.zeros_like(near)
 
     def near_tile(source_t, source_chg, keep, mirror=None):
         def body(step, carry):
@@ -383,6 +375,14 @@
     arrive("first")
     raise_first()
     send_first()
+    for row in range(0, LEAF, CHUNK):
+        pts_t[row : row + CHUNK, :] = jnp.transpose(pts[:, row : row + CHUNK])
+    exchange("p0", pts_t, near_pts.at[0], near_pts.at[0], partner)
+    exchange("p1", ordered, near_chg.at[0], near_chg.at[0], partner)
+    send_pieces(PIECES[0])
+    wide = pts[...].astype(F32)
+    norm_t[...] = jnp.sum(wide * wide, axis=0, keepdims=True) * SCALE
+    near[...] = jnp.zeros_like(near)
     send_pieces(PIECES[1])
     arrive("first rest")
     raise_rest(0)
@@ -402,16 +402,9 @@
     keep_cousins(2, coords_far)
     spread(2)
     spread(3)
-    for index in range(N_PIECE):
-        arrive(("near", index))
-    for name, ref in (("f0", near_pts), ("f1", near_chg)):
-        exchange(name, ref.at[1], ref.at[2], ref.at[2], partner, from_there, to_there)
-
-    @pl.when(from_there)
-    def _():
-        near_tile(near_pts.at[1], near_chg.at[1], keep_in, back.at[0])
-
-    exchange("back", back.at[0], back.at[1], back.at[1], backward, from_there, to_there)
+    arrive("p0")
+    arrive("p1")
+    near_tile(near_pts.at[0], near_chg.at[0], keep_p)
 
     joined, weights, coords_far = raise_family(4)
     bundle[LEVELS, COORD:WEIGHT] = joined
@@ -430,9 +423,16 @@
     spread(5)
     spread_side(2)
     spread_side(3)
-    arrive("p0")
-    arrive("p1")
-    near_tile(near_pts.at[0], near_chg.at[0], keep_p)
+    for index in range(N_PIECE):
+        arrive(("near", index))
+    for name, ref in (("f0", near_pts), ("f1", near_chg)):
+        exchange(name, ref.at[1], ref.at[2], ref.at[2], partner, from_there, to_there)
+
+    @pl.when(from_there)
+    def _():
+        near_tile(near_pts.at[1], near_chg.at[1], keep_in, back.at[0])
+
+    exchange("back", back.at[0], back.at[1], back.at[1], backward, from_there, to_there)
     complete(2)
     complete(3)
 

time: 50 us -> 49.4 us (0.988)
  Pallas kernels: 47.7 us -> 47.1 us
    pallas_call x1, Pallas kernels: 47.7 us -> 47.1 us  [local(): pl.pallas_call(functools.partial(kernel, n_y, n_x, n_grp), out_shape=jax....]
where the time goes in v4:
time: 49.4 us; the launch traced here: 48.8 us
  Pallas kernels  47.1 us (95%)
  local copies, waits for them, and re-layouts  1.67 us (3%)
    pallas_call x1, Pallas kernels, local(): pl.pallas_call(functools.partial(kernel, n_y, n_x, n_grp), out_shape=jax....  47.1 us
    unnamed x1, local copies, waits for them, and re-layouts  1.67 us

profile of v4, /device:TPU:1, one launch (start us, length us, event | category | flops | bytes accessed | tf_op | source)
XLA Modules:
  0.0 48.8 jit_solution(7067036406624758540)
XLA Ops:
  0.0 47.1 %shard_map.73 = f32[64,1024]{1,0:T(8,128)} custom-call(bf16[256,1024]{1,0:T(8,128)(2,1)} %points_hbm.1, bf16[64,1024]{1,0:T(8,128)(2,1)} %charges_hbm.1, s32[1,1024]{1,0:T(1,128)} %bitcast.4, s32[1,5]{1,0:T(1,128)} %mask_ref.1, s32[7,1,128]{2,1,0:T(1,128)} %bitcast.5, bf16[128,1024]{1,0:T(8,128)(2,1)} %interp_hbm.1, bf16[6,128,128]{2,1,0:T(8,128)(2,1)} %bitcast.3), custom_call_target="tpu_custom_call" | custom-call | tf_op jit(solution)/shard_map/pallas_call | solution.py:498
  47.1 1.7 %copy.9 = f32[64,1024]{1,0:T(8,128)} copy(f32[64,1024]{1,0:T(8,128)} %shard_map.73) | data formatting | bytes 524288

commit v5 on v4

--- a/solution.py
+++ b/solution.py
@@ -447,22 +447,16 @@
         source = top.at[step - 1, diagonal]
         exchange(("top corner", step), source, source, top.at[step - 1, corner], partner)
 
-    arrive("f0")
-    arrive("f1")
-
-    @pl.when(to_there)
-    def _():
-        near_tile(near_pts.at[2], near_chg.at[2], keep_f)
-
     for step in steps:
         top_spread(step)
     spread_side(4)
     spread_side(5)
-    arrive("back")
+    arrive("f0")
+    arrive("f1")
 
     @pl.when(to_there)
     def _():
-        near[...] += jnp.where(keep_out > 0, back[1], 0.0)
+        near_tile(near_pts.at[2], near_chg.at[2], keep_f)
 
     for step in steps:
         top_spread_side(step)
@@ -484,6 +478,12 @@
 
     for level in range(LEVELS - 1, -1, -1):
         potential = times(potential, transfer[level]) + far[level]
+    arrive("back")
+
+    @pl.when(to_there)
+    def _():
+        near[...] += jnp.where(keep_out > 0, back[1], 0.0)
+
     out_ref[...] = near[...] + times(potential, interp[...])
     finish()
 

time: 49.4 us -> 49.1 us (level)
  no operation moved by 1% of the time
where the time goes in v5:
time: 49.1 us; the launch traced here: 49 us
  Pallas kernels  47.3 us (96%)
  local copies, waits for them, and re-layouts  1.67 us (3%)
    pallas_call x1, Pallas kernels, local(): pl.pallas_call(functools.partial(kernel, n_y, n_x, n_grp), out_shape=jax....  47.3 us
    unnamed x1, local copies, waits for them, and re-layouts  1.67 us

profile of v5, /device:TPU:1, one launch (start us, length us, event | category | flops | bytes accessed | tf_op | source)
XLA Modules:
  0.0 49.0 jit_solution(12270406094137357400)
XLA Ops:
  0.0 47.3 %shard_map.73 = f32[64,1024]{1,0:T(8,128)} custom-call(bf16[256,1024]{1,0:T(8,128)(2,1)} %points_hbm.1, bf16[64,1024]{1,0:T(8,128)(2,1)} %charges_hbm.1, s32[1,1024]{1,0:T(1,128)} %bitcast.4, s32[1,5]{1,0:T(1,128)} %mask_ref.1, s32[7,1,128]{2,1,0:T(1,128)} %bitcast.5, bf16[128,1024]{1,0:T(8,128)(2,1)} %interp_hbm.1, bf16[6,128,128]{2,1,0:T(8,128)(2,1)} %bitcast.3), custom_call_target="tpu_custom_call" | custom-call | tf_op jit(solution)/shard_map/pallas_call | solution.py:498
  47.3 1.7 %copy.9 = f32[64,1024]{1,0:T(8,128)} copy(f32[64,1024]{1,0:T(8,128)} %shard_map.73) | data formatting | bytes 524288

commit v6 on v5

--- a/solution.py
+++ b/solution.py
@@ -433,8 +433,6 @@
         near_tile(near_pts.at[1], near_chg.at[1], keep_in, back.at[0])
 
     exchange("back", back.at[0], back.at[1], back.at[1], backward, from_there, to_there)
-    complete(2)
-    complete(3)
 
     def top_spread(step):
         arrive(("top", step))
@@ -451,6 +449,8 @@
         top_spread(step)
     spread_side(4)
     spread_side(5)
+    complete(2)
+    complete(3)
     arrive("f0")
     arrive("f1")
 

time: 49.1 us -> 49.6 us (1.010)
  Pallas kernels: 47.3 us -> 47.8 us
where the time goes in v6:
time: 49.6 us; the launch traced here: 49.4 us
  Pallas kernels  47.8 us (96%)
  local copies, waits for them, and re-layouts  1.67 us (3%)
    pallas_call x1, Pallas kernels, local(): pl.pallas_call(functools.partial(kernel, n_y, n_x, n_grp), out_shape=jax....  47.8 us
    unnamed x1, local copies, waits for them, and re-layouts  1.67 us

profile of v6, /device:TPU:1, one launch (start us, length us, event | category | flops | bytes accessed | tf_op | source)
XLA Modules:
  0.0 49.4 jit_solution(12025804566464622882)
XLA Ops:
  0.0 47.8 %shard_map.73 = f32[64,1024]{1,0:T(8,128)} custom-call(bf16[256,1024]{1,0:T(8,128)(2,1)} %points_hbm.1, bf16[64,1024]{1,0:T(8,128)(2,1)} %charges_hbm.1, s32[1,1024]{1,0:T(1,128)} %bitcast.4, s32[1,5]{1,0:T(1,128)} %mask_ref.1, s32[7,1,128]{2,1,0:T(1,128)} %bitcast.5, bf16[128,1024]{1,0:T(8,128)(2,1)} %interp_hbm.1, bf16[6,128,128]{2,1,0:T(8,128)(2,1)} %bitcast.3), custom_call_target="tpu_custom_call" | custom-call | tf_op jit(solution)/shard_map/pallas_call | solution.py:498
  47.8 1.7 %copy.9 = f32[64,1024]{1,0:T(8,128)} copy(f32[64,1024]{1,0:T(8,128)} %shard_map.73) | data formatting | bytes 524288
